TPU v7x, 32 devices: a whole 2x2x4 slice. The times are simulated.
32 devices in a mesh: seq: 4 (over z), head: 2 (over core), batch: 4 (over y, x).
Axes of the slice: x: 2, y: 2, z: 4, core: 2. Of those that a mesh axis runs over, the one named last changes fastest.
Arguments:
- tokens: bfloat16 [8, 4096, 1024], P('batch', 'seq'), may hold values from -6 to 6
- cotangent: bfloat16 [8, 4096, 1024], P('batch', 'seq'), may hold values from -6 to 6
- adapter_index: int32 [8], P('batch'), may hold values from 0 to 7
- norm_gain: float32 [1024], replicated, may hold values from 0.5 to 1.5
- gate_input_weight: bfloat16 [1024, 2, 2048], P(None, None, 'head'), may hold values from -0.1875 to 0.1875
- bc_weight: bfloat16 [1024, 2, 128], P(None, None, 'head'), may hold values from -0.1875 to 0.1875
- step_weight: bfloat16 [1024, 32], P(None, 'head'), may hold values from -0.1875 to 0.1875
- conv_x: float32 [5, 2048], P(None, 'head'), may hold values from -0.6 to 0.6
- conv_bc: float32 [5, 2, 128], P(None, None, 'head'), may hold values from -0.6 to 0.6
- dt_bias: float32 [32], P('head'), may hold values from -6 to -2
- a_log: float32 [32], P('head'), may hold values from -4.6 to 2
- skip_gain: float32 [32], P('head'), may hold values from 0.5 to 1.5
- out_gain: float32 [2048], P('head'), may hold values from 0.5 to 1.5
- output_weight: bfloat16 [2048, 1024], P('head'), may hold values from -0.125 to 0.125
- in_down: bfloat16 [8, 1024, 16], replicated, may hold values from -0.1875 to 0.1875
- in_up: bfloat16 [8, 16, 2, 2048], P(None, None, None, 'head'), may hold values from -0.8984375 to 0.8984375
- out_down: bfloat16 [8, 2048, 16], P(None, 'head'), may hold values from -0.125 to 0.125
- out_up: bfloat16 [8, 16, 1024], replicated, may hold values from -0.8984375 to 0.8984375
Outputs:
- result: bfloat16 [8, 4096, 1024], P('batch', 'seq', 'head')
- grad_tokens: bfloat16 [8, 4096, 1024], P('batch', 'seq', 'head')
- grad_in_down: float32 [8, 1024, 16], replicated
- grad_in_up: float32 [8, 16, 2, 2048], P(None, None, None, 'head')
- grad_out_down: float32 [8, 2048, 16], P(None, 'head')
- grad_out_up: float32 [8, 16, 1024], replicated
All inputs are finite; a program needn't handle non-finite values.
Results may differ from a plain program's by a relative error of at most 0.0035.
The roundings to bfloat16 on the way count: a program that leaves them out, or rounds other values in their place, can miss the bound.
Values may be sent and summed in bfloat16 or wider, within the bound.
A program may use at most 256 MiB of HBM per device.

v0:
```python
import jax
import jax.numpy as jnp
from jax import lax
from jax.sharding import PartitionSpec as P

STRETCH = 256


EPSILON = 1e-05
EXACT_MATMUL = lax.Precision.HIGHEST


def passed_along(x, axis, by):
    count = lax.axis_size(axis)
    pairs = [(i, i + by) for i in range(count) if 0 <= i + by < count]
    return lax.ppermute(x, axis, pairs)


def entering(value, axis, join, neutral, backward):
    count, mine = (lax.axis_size(axis), lax.axis_index(axis))
    pieces = jax.tree.map(lambda part: lax.all_gather(part, axis), value)
    if backward:
        pieces = jax.tree.map(lambda part: part[::-1], pieces)
        mine = count - 1 - mine
    running = jax.tree.map(
        lambda part, zero: jnp.full_like(part, 0) + jnp.asarray(zero, part.dtype), value, neutral
    )

    def step(position, running):
        longer = join(running, jax.tree.map(lambda part: part[position], pieces))
        return jax.tree.map(lambda new, old: jnp.where(position < mine, new, old), longer, running)

    return lax.fori_loop(0, count - 1, step, running)


def conv_apply(extended, tap_table, length):
    tap_span = tap_table.shape[0] - 1
    summed = tap_table[tap_span]
    for tap_index in range(tap_span):
        summed = summed + tap_table[tap_index] * extended[:, tap_index : tap_index + length]
    return summed


def conv_reverse(grad_pre, tap_table):
    tap_span = tap_table.shape[0] - 1
    summed = jnp.zeros(
        (grad_pre.shape[0], grad_pre.shape[1] + tap_span - 1) + grad_pre.shape[2:], jnp.float32
    )
    extra = [(0, 0)] * (grad_pre.ndim - 2)
    for tap_index in range(tap_span):
        widths = [(0, 0), (tap_index, tap_span - 1 - tap_index)] + extra
        summed = summed + jnp.pad(tap_table[tap_index] * grad_pre, widths)
    return summed


def silu_slope(values):
    sigma = jax.nn.sigmoid(values)
    return sigma * (1.0 + values * (1.0 - sigma))


def end_state(head_input, b_val, step_size, log_decay):
    running = jnp.cumsum(log_decay, 1)
    tail_weight = jnp.exp(running[:, -1:] - running) * step_size
    leaving = jnp.einsum(
        "slh,slhp,sln->shpn", tail_weight, head_input, b_val, precision=EXACT_MATMUL
    )
    return (leaving, jnp.exp(running[:, -1]))


def local_scan(head_input, b_val, c_val, step_size, log_decay, incoming):
    seq_count = head_input.shape[0]
    length = head_input.shape[1]
    block_len = min(STRETCH, length)
    block_count = length // block_len
    places = jnp.arange(block_len)
    allowed = (places[:, None] >= places[None, :])[None, :, :, None]

    def one_block(carry_state, pieces):
        x_block, b_block, c_block, step_block, log_block = pieces
        running = jnp.cumsum(log_block, 1)
        spread = jnp.where(allowed, running[:, :, None, :] - running[:, None, :, :], -jnp.inf)
        scores = jnp.einsum("stn,sun->stu", c_block, b_block, precision=EXACT_MATMUL)
        weights = jnp.exp(spread) * scores[..., None] * step_block[:, None, :, :]
        within = jnp.einsum("stuh,suhp->sthp", weights, x_block, precision=EXACT_MATMUL)
        carried = jnp.exp(running)[..., None] * jnp.einsum(
            "stn,shpn->sthp", c_block, carry_state, precision=EXACT_MATMUL
        )
        tail_weight = jnp.exp(running[:, -1:] - running) * step_block
        new_state = jnp.exp(running[:, -1])[:, :, None, None] * carry_state + jnp.einsum(
            "suh,suhp,sun->shpn", tail_weight, x_block, b_block, precision=EXACT_MATMUL
        )
        return (new_state, within + carried)

    pieces = tuple(
        (
            jnp.moveaxis(v.reshape((seq_count, block_count, block_len) + v.shape[2:]), 1, 0)
            for v in (head_input, b_val, c_val, step_size, log_decay)
        )
    )
    _, scanned = lax.scan(jax.checkpoint(one_block), incoming, pieces)
    return jnp.moveaxis(scanned, 0, 1).reshape(head_input.shape)


def chain(earlier, later):
    return (earlier[0] * later[0], later[0][:, :, None, None] * earlier[1] + later[1])


def local(
    tokens,
    cotangent,
    adapter_index,
    norm_gain,
    gate_input_weight,
    bc_weight,
    step_weight,
    conv_x,
    conv_bc,
    dt_bias,
    a_log,
    skip_gain,
    out_gain,
    output_weight,
    in_down,
    in_up,
    out_down,
    out_up,
):
    seq_count, length, model_width = tokens.shape
    head_count = dt_bias.shape[0]
    inner_width = output_weight.shape[0]
    head_size = inner_width // head_count
    half_width = model_width // lax.axis_size("head")
    head_part = lax.axis_index("head")
    full_inner = inner_width * lax.axis_size("head")
    conv_lag = conv_x.shape[0] - 2
    half_float = jnp.bfloat16
    full_float = jnp.float32
    chosen = (adapter_index[:, None] == jnp.arange(in_down.shape[0])[None, :]).astype(full_float)
    chosen_input_down = jnp.einsum("sa,adr->sdr", chosen, in_down.astype(full_float))
    pick_in_up = jnp.einsum("sa,arki->srki", chosen, in_up.astype(full_float))
    pick_out_down = jnp.einsum("sa,air->sir", chosen, out_down.astype(full_float))
    chosen_output_up = jnp.einsum("sa,ard->srd", chosen, out_up.astype(full_float))
    tokens_f = tokens.astype(full_float)
    scale_in = lax.rsqrt(jnp.mean(tokens_f * tokens_f, -1, keepdims=True) + EPSILON)
    normalized_rows = (tokens_f * scale_in * norm_gain).astype(half_float)
    lowrank_product = jnp.einsum(
        "bij,bjg->big",
        normalized_rows,
        chosen_input_down.astype(half_float),
        preferred_element_type=full_float,
    )
    projected_rows = jnp.einsum(
        "tbh,hna->tbna", normalized_rows, gate_input_weight, preferred_element_type=full_float
    )
    projected_rows = (
        projected_rows
        + jnp.einsum("slr,srki->slki", lowrank_product, pick_in_up, precision=EXACT_MATMUL)
    ).astype(half_float)
    raw_bc_values = jnp.einsum(
        "ouh,hcm->oucm", normalized_rows, bc_weight, preferred_element_type=full_float
    ).astype(half_float)
    raw_step_sizes = jnp.einsum(
        "vyo,ou->vyu", normalized_rows, step_weight, preferred_element_type=full_float
    ).astype(half_float)
    x_raw = projected_rows[:, :, 1]
    x_before, bc_before = passed_along(
        (x_raw[:, length - conv_lag :], raw_bc_values[:, length - conv_lag :]), "seq", 1
    )
    x_pre = conv_apply(jnp.concatenate([x_before, x_raw], 1).astype(full_float), conv_x, length)
    bc_pre = conv_apply(
        jnp.concatenate([bc_before, raw_bc_values], 1).astype(full_float), conv_bc, length
    )
    x_conv = jax.nn.silu(x_pre).astype(half_float)
    bc_conv = jax.nn.silu(bc_pre).astype(half_float)
    bc_full = lax.all_gather(bc_conv, "head", axis=3, tiled=True)
    a_rate = -jnp.exp(a_log)
    dt_in = raw_step_sizes.astype(full_float) + dt_bias
    step_size = jax.nn.softplus(dt_in)
    log_decay = step_size * a_rate
    head_input = x_conv.astype(full_float).reshape(seq_count, length, head_count, head_size)
    b_val = bc_full[:, :, 0].astype(full_float)
    c_val = bc_full[:, :, 1].astype(full_float)
    (leaving, decay_all), pull_end = jax.vjp(end_state, head_input, b_val, step_size, log_decay)
    neutral = (jnp.ones_like(decay_all), jnp.zeros_like(leaving))
    _, incoming = entering((decay_all, leaving), "seq", chain, neutral, False)
    scanned, pull_scan = jax.vjp(
        local_scan, head_input, b_val, c_val, step_size, log_decay, incoming
    )
    y_val = (scanned + skip_gain[:, None] * head_input).reshape(seq_count, length, inner_width)
    gate_val = projected_rows[:, :, 0].astype(full_float)
    gate_act = jax.nn.silu(gate_val)
    gated = y_val * gate_act
    squares = lax.psum(jnp.sum(gated * gated, -1), "head")
    scale_out = lax.rsqrt(squares / full_inner + EPSILON)[..., None]
    norm_output = (gated * scale_out * out_gain).astype(half_float)
    down_portion = jnp.einsum(
        "sli,sir->slr",
        norm_output,
        pick_out_down.astype(half_float),
        preferred_element_type=full_float,
    )
    partial_output = jnp.einsum(
        "fgc,cj->fgj", norm_output, output_weight, preferred_element_type=full_float
    )
    partial_output = partial_output + jnp.einsum(
        "hab,hbe->hae", down_portion, chosen_output_up, precision=EXACT_MATMUL
    )
    mixed = lax.psum_scatter(partial_output, "head", scatter_dimension=2, tiled=True)
    own_tokens = lax.dynamic_slice_in_dim(tokens_f, head_part * half_width, half_width, 2)
    result = (own_tokens + mixed).astype(half_float)
    back_lowrank = jnp.einsum(
        "gip,gvp->giv",
        cotangent,
        chosen_output_up.astype(half_float),
        preferred_element_type=full_float,
    )
    norm_output_gradient = jnp.einsum(
        "pqt,wt->pqw", cotangent, output_weight, preferred_element_type=full_float
    )
    norm_output_gradient = norm_output_gradient + jnp.einsum(
        "slr,sir->sli", back_lowrank, pick_out_down, precision=EXACT_MATMUL
    )
    seq_out_down = jnp.einsum(
        "sli,slr->sir", norm_output.astype(full_float), back_lowrank, precision=EXACT_MATMUL
    )
    sequence_output_up = jnp.einsum(
        "vhg,vhp->vgp", down_portion, cotangent.astype(full_float), precision=EXACT_MATMUL
    )
    weighted_out = norm_output_gradient * out_gain
    inner_total = lax.psum(jnp.sum(weighted_out * gated, -1), "head")
    grad_gated = (
        scale_out * weighted_out - gated * scale_out**3 * (inner_total / full_inner)[..., None]
    )
    grad_y = (grad_gated * gate_act).reshape(seq_count, length, head_count, head_size)
    grad_gate = grad_gated * y_val * silu_slope(gate_val)
    grad_x1, grad_b1, grad_c1, grad_dt1, grad_log1, grad_in_state = pull_scan(grad_y)
    _, returned = entering((decay_all, grad_in_state), "seq", chain, neutral, True)
    grad_decay = jnp.sum(returned * incoming, (2, 3))
    grad_x2, grad_b2, grad_dt2, grad_log2 = pull_end((returned, grad_decay))
    grad_head = grad_x1 + grad_x2 + skip_gain[:, None] * grad_y
    grad_step = grad_dt1 + grad_dt2 + (grad_log1 + grad_log2) * a_rate
    raw_step_gradient = (grad_step * jax.nn.sigmoid(dt_in)).astype(half_float)
    grad_bc = lax.psum_scatter(
        jnp.stack([grad_b1 + grad_b2, grad_c1], 2), "head", scatter_dimension=3, tiled=True
    )
    x_back = conv_reverse(
        grad_head.reshape(seq_count, length, inner_width) * silu_slope(x_pre), conv_x
    )
    bc_back = conv_reverse(grad_bc * silu_slope(bc_pre), conv_bc)
    x_after, bc_after = passed_along((x_back[:, :conv_lag], bc_back[:, :conv_lag]), "seq", -1)
    grad_x_raw = x_back[:, conv_lag:].at[:, length - conv_lag :].add(x_after)
    raw_bc_gradient = (
        bc_back[:, conv_lag:].at[:, length - conv_lag :].add(bc_after).astype(half_float)
    )
    projection_gradient = jnp.stack([grad_gate, grad_x_raw], 2).astype(half_float)
    lowrank_gradient = jnp.einsum(
        "slki,srki->slr",
        projection_gradient,
        pick_in_up.astype(half_float),
        preferred_element_type=full_float,
    )
    norm_portion_gradient = jnp.einsum(
        "wevr,nvr->wen", projection_gradient, gate_input_weight, preferred_element_type=full_float
    )
    norm_portion_gradient = norm_portion_gradient + jnp.einsum(
        "ozgv,pgv->ozp", raw_bc_gradient, bc_weight, preferred_element_type=full_float
    )
    norm_portion_gradient = norm_portion_gradient + jnp.einsum(
        "gui,bi->gub", raw_step_gradient, step_weight, preferred_element_type=full_float
    )
    norm_portion_gradient = norm_portion_gradient + jnp.einsum(
        "kao,kxo->kax", lowrank_gradient, chosen_input_down, precision=EXACT_MATMUL
    )
    seq_in_up = jnp.einsum(
        "slr,slki->srki",
        lowrank_product,
        projection_gradient.astype(full_float),
        precision=EXACT_MATMUL,
    )
    sequence_input_down = jnp.einsum(
        "iwm,iwz->imz", normalized_rows.astype(full_float), lowrank_gradient, precision=EXACT_MATMUL
    )
    own_cot = lax.dynamic_slice_in_dim(cotangent, head_part * half_width, half_width, 2).astype(
        full_float
    )
    grad_norm = lax.psum(norm_portion_gradient, "head")
    weighted_in = grad_norm * norm_gain
    input_stat = jnp.sum(weighted_in * tokens_f, -1, keepdims=True)
    grad_full = scale_in * weighted_in - tokens_f * scale_in**3 * input_stat / model_width
    grad_own = lax.dynamic_slice_in_dim(grad_full, head_part * half_width, half_width, 2)
    grad_tokens = (own_cot + grad_own).astype(half_float)
    local_sums = (
        jnp.einsum("sa,srki->arki", chosen, seq_in_up, precision=EXACT_MATMUL),
        jnp.einsum("sa,sir->air", chosen, seq_out_down, precision=EXACT_MATMUL),
    )
    shared_sums = (
        jnp.einsum("sa,sdr->adr", chosen, sequence_input_down, precision=EXACT_MATMUL),
        jnp.einsum("sa,srd->ard", chosen, sequence_output_up, precision=EXACT_MATMUL),
    )
    grad_in_up, grad_out_down = lax.psum((local_sums[0], local_sums[1]), ("seq", "batch"))
    grad_in_down, grad_out_up = lax.psum((shared_sums[0], shared_sums[1]), ("seq", "head", "batch"))
    return (result, grad_tokens, grad_in_down, grad_in_up, grad_out_down, grad_out_up)


def solution(mesh):
    in_specs = (
        P("batch", "seq", None),
        P("batch", "seq", None),
        P("batch"),
        P(),
        P(None, None, "head"),
        P(None, None, "head"),
        P(None, "head"),
        P(None, "head"),
        P(None, None, "head"),
        P("head"),
        P("head"),
        P("head"),
        P("head"),
        P("head", None),
        P(),
        P(None, None, None, "head"),
        P(None, "head", None),
        P(),
    )
    out_specs = (
        P("batch", "seq", "head"),
        P("batch", "seq", "head"),
        P(),
        P(None, None, None, "head"),
        P(None, "head", None),
        P(),
    )
    return jax.shard_map(local, mesh=mesh, in_specs=in_specs, out_specs=out_specs, check_vma=False)
```

profile of v0, /device:TPU:0, one launch (start us, length us, event | category | flops | bytes accessed | tf_op | source)
XLA Modules:
  0.0 1424.2 jit_solution(9138751716288617538)
XLA Ops:
  19.2 16.0 %fusion.162 = f32[2,1024,2,1024]{3,1,2,0:T(8,128)} fusion(f32[2,1024,16,1]{1,2,3,0:T(8,128)S(1)} %convolution_bitcast_fusion.1, f32[2,16,2,1024]{3,0,2,1:T(2,128)S(1)} %get-tuple-element.1051), kind=kOutput, calls=%fused_computation.267 | convolution fusion | flops 805306368 | bytes 17170432 | tf_op jit(solution)/shard_map/slr,srki->slki/dot_general | solution.py:157
  35.2 15.9 %add_convert_fusion = bf16[2,1024,2,1024]{3,1,2,0:T(8,128)(2,1)} fusion(f32[2,1024,2,1024]{3,1,2,0:T(8,128)} %fusion.162, bf16[1024,2,1024]{2,1,0:T(2,128)(2,1)} %param.34, bf16[2,1024,1024]{2,1,0:T(8,128)(2,1)S(1)} %copy-done.7, f32[1024]{0:T(1024)S(1)} %copy-done.73, f32[2,1024]{1,0:T(2,128)S(1)} %get-tuple-element.1042), kind=kOutput, calls=%fused_computation.127 | convolution fusion | flops 8606711808 | bytes 33566720 | tf_op jit(solution)/shard_map/tbh,hna->tbna/dot_general | solution.py:152
  77.1 9.0 reduce-window.78
  95.7 6.8 maximum_convert_fusion
  102.5 17.6 %multiply_convert_fusion.1 = (bf16[2,1024,1024]{2,1,0:T(8,128)(2,1)}, f32[2,1024,1024]{2,1,0:T(8,128)}) fusion(f32[2,1027,1024]{2,1,0:T(8,128)} %maximum_convert_fusion, f32[1024]{0:T(1024)S(1)} %bitcast.600, f32[1024]{0:T(1024)S(1)} %bitcast.602, f32[1024]{0:T(1024)S(1)} %bitcast.598, f32[1024]{0:T(1024)S(1)} %bitcast.604, f32[1024]{0:T(1024)S(1)} %bitcast.608), kind=kLoop, calls=%fused_computation.168 | loop fusion | flops 27262976 | bytes 46157824 | tf_op jit(solution)/shard_map/convert_element_type | solution.py:173
  120.1 6.2 copy.371
  126.4 7.5 fusion.90
  137.5 9.5 all-gather
  154.2 9.1 fusion.122
  163.3 7.0 copy.374
  170.3 10.6 reshape_reshape.6
  180.9 8.4 copy.378
  201.4 13.1 all-gather.9.cloned.1.call-done
  225.6 97.5 %while.71 = (s32[]{:T(128)}, f32[2,16,64,128]{3,2,1,0:T(8,128)S(1)}, f32[4,2,256,16,64]{2,4,3,1,0:T(8,128)}, f32[4,2,16,64,128]{4,3,2,1,0:T(8,128)}, f32[4,2,256...) while((s32[]{:T(128)}, ...), condition=%wide.region_8.9_spmd.clone, body=%wide.region_5.8_spmd.clone.sunk | while | flops 3434110976 | bytes 18423296 | solution.py:100
  230.1 11.1 fusion.297
  254.3 11.1 fusion.297
  278.6 11.1 fusion.297
  302.9 11.1 fusion.297
  323.1 14.5 %copy.447 = f32[2,4,256,16,64]{4,3,2,1,0:T(8,128)} copy(f32[2,4,256,16,64]{2,4,3,0,1:T(8,128)} %bitcast.578) | data formatting | bytes 16777216 | tf_op jit(solution)/shard_map/jvp()/reshape | solution.py:101
  337.6 14.5 %reshape.422 = f32[2,1024,1024]{2,1,0:T(8,128)} reshape(f32[2,4,256,16,64]{4,3,2,1,0:T(8,128)} %copy.447) | data formatting | bytes 16777216 | tf_op jit(solution)/shard_map/jvp()/reshape | solution.py:101
  352.1 19.6 %multiply_reduce_fusion.5 = (f32[2,1024]{1,0:T(2,128)S(1)}, f32[2,1024]{1,0:T(2,128)S(1)}, f32[2,1024,1024]{2,1,0:T(8,128)}, f32[2,1024,1024]{2,1,0:T(8,128)}) fusion(bf16[2,1024,2,1024]{3,1,2,0:T(8,128)(2,1)} %add_convert_fusion, f32[2,1024,1024]{2,1,0:T(8,128)} %reshape.422, bf16[2,1024,1024]{2,1,0:T(8,128)(2,1)} %get-tuple-element.1005, ...), kind=kOutput, calls=%fused_computation.163 | convolution fusion | flops 434106368 | bytes 42229760 | tf_op jit(solution)/shard_map/slr,sir->sli/dot_general | solution.py:220
  375.0 19.5 %fusion.119 = (bf16[2,1024,1,1024]{3,1,0,2:T(8,128)(2,1)}, f32[2,1024,1024]{2,1,0:T(8,128)}, bf16[2,1024,1024]{2,1,0:T(8,128)(2,1)}) fusion(bf16[2,1024,2,1024]{3,1,2,0:T(8,128)(2,1)} %add_convert_fusion, f32[2,1024,1024]{2,1,0:T(8,128)} %reshape.422, f32[1024]{0:T(1024)S(1)} %mul.690, bf16[2,1024,1024]{2,1,0:T(8,128)(2,1)} %get-tuple-element.1005, ...), kind=kLoop, calls=%fused_computation.196 | loop fusion | flops 48234496 | bytes 50364416 | tf_op jit(solution)/shard_map/stack | solution.py:255
  394.6 8.7 copy.389
  403.3 10.5 reshape_reshape.7
  422.3 421.9 %while.73 = (s32[]{:T(128)}, f32[2,16,64,128]{3,2,1,0:T(8,128)}, f32[4,2,256,16,64]{2,4,3,1,0:T(8,128)}, f32[4,2,256,128]{3,2,1,0:T(8,128)}, f32[4,2,256,128]{3,...) while((s32[]{:T(128)}, f32[2,16,64,128]{3,2,1,0:T(8,128)}, ...), condition=%wide.region_26.27_spmd.clone, body=%wide.region_14.26_spmd.clone.sunk | while | flops 7895670784 | bytes 70031112 | solution.py:100
  442.3 5.6 constant_dynamic-slice_fusion.2
  478.6 15.3 %fusion.319 = (f32[2,256,16]{1,2,0:T(8,128)}, f32[2,256,16]{1,2,0:T(8,128)}, f32[2,256,16]{1,2,0:T(8,128)}, f32[2,256,256]{2,1,0:T(8,128)}) fusion(f32[2,256,16]{1,2,0:T(8,128)S(1)} %copy.568, f32[2,256,256]{2,1,0:T(8,128)} %fusion.318, f32[2,256,16]{1,2,0:T(8,128)S(1)} %copy.570, pred[256,256]{1,0:T(8,128)(4,1)} %bitcast.592, ...), kind=kOutput, calls=%fused_computation.62.clone.1 | convolution fusion | flops 1637720064 | bytes 5472256 | tf_op jit(solution)/shard_map/transpose(jvp())/while/body/eval_jaxpr/checkpoint/stuh,suhp->sthp/dot_general | solution.py:84
  511.9 5.3 fusion.325
  528.8 10.0 bitcast_dynamic-update-slice_fusion.10
  541.8 5.6 constant_dynamic-slice_fusion.2
  579.3 15.3 %fusion.319 = (f32[2,256,16]{1,2,0:T(8,128)}, f32[2,256,16]{1,2,0:T(8,128)}, f32[2,256,16]{1,2,0:T(8,128)}, f32[2,256,256]{2,1,0:T(8,128)}) fusion(f32[2,256,16]{1,2,0:T(8,128)S(1)} %copy.568, f32[2,256,256]{2,1,0:T(8,128)} %fusion.318, f32[2,256,16]{1,2,0:T(8,128)S(1)} %copy.570, pred[256,256]{1,0:T(8,128)(4,1)} %bitcast.592, ...), kind=kOutput, calls=%fused_computation.62.clone.1 | convolution fusion | flops 1637720064 | bytes 5472256 | tf_op jit(solution)/shard_map/transpose(jvp())/while/body/eval_jaxpr/checkpoint/stuh,suhp->sthp/dot_general | solution.py:84
  612.6 5.3 fusion.325
  629.5 10.0 bitcast_dynamic-update-slice_fusion.10
  642.5 5.6 constant_dynamic-slice_fusion.2
  680.0 15.3 %fusion.319 = (f32[2,256,16]{1,2,0:T(8,128)}, f32[2,256,16]{1,2,0:T(8,128)}, f32[2,256,16]{1,2,0:T(8,128)}, f32[2,256,256]{2,1,0:T(8,128)}) fusion(f32[2,256,16]{1,2,0:T(8,128)S(1)} %copy.568, f32[2,256,256]{2,1,0:T(8,128)} %fusion.318, f32[2,256,16]{1,2,0:T(8,128)S(1)} %copy.570, pred[256,256]{1,0:T(8,128)(4,1)} %bitcast.592, ...), kind=kOutput, calls=%fused_computation.62.clone.1 | convolution fusion | flops 1637720064 | bytes 5472256 | tf_op jit(solution)/shard_map/transpose(jvp())/while/body/eval_jaxpr/checkpoint/stuh,suhp->sthp/dot_general | solution.py:84
  730.2 10.0 bitcast_dynamic-update-slice_fusion.10
  743.1 5.6 constant_dynamic-slice_fusion.2
  780.7 15.3 %fusion.319 = (f32[2,256,16]{1,2,0:T(8,128)}, f32[2,256,16]{1,2,0:T(8,128)}, f32[2,256,16]{1,2,0:T(8,128)}, f32[2,256,256]{2,1,0:T(8,128)}) fusion(f32[2,256,16]{1,2,0:T(8,128)S(1)} %copy.568, f32[2,256,256]{2,1,0:T(8,128)} %fusion.318, f32[2,256,16]{1,2,0:T(8,128)S(1)} %copy.570, pred[256,256]{1,0:T(8,128)(4,1)} %bitcast.592, ...), kind=kOutput, calls=%fused_computation.62.clone.1 | convolution fusion | flops 1637720064 | bytes 5472256 | tf_op jit(solution)/shard_map/transpose(jvp())/while/body/eval_jaxpr/checkpoint/stuh,suhp->sthp/dot_general | solution.py:84
  813.9 5.3 fusion.325
  830.9 9.9 bitcast_dynamic-update-slice_fusion.10
  844.3 8.3 copy.482
  876.6 47.0 %all-gather.11.cloned.1.call-done = f32[8,16,64,128]{3,2,1,0:T(8,128)} async-done(((f32[2,16,64,128]{3,2,1,0:T(8,128)}), f32[8,16,64,128]{3,2,1,0:T(8,128)}) %all-gather.11.cloned.1.call-update) | async-done | bytes 4194320 | tf_op jit(solution)/shard_map/all_gather | solution.py:21
  932.9 11.9 fusion.91
  944.8 8.7 copy.396
  953.5 9.7 broadcast_multiply_fusion.3
  963.2 14.2 broadcast_multiply_fusion.2
  978.3 13.1 pad_add_fusion
  993.1 7.2 fusion.128
  1009.9 39.6 %reduce-window.80 = f32[2,16,8,128]{3,2,1,0:T(8,128)S(1)} reduce-window(f32[2,16,8,128]{3,2,1,0:T(8,128)S(1)} %copy.402, f32[]{:T(128)} %constant.247.clone.1), window={size=1x1x1x128 pad=0_0x0_0x0_0x0_127}, to_apply=%region_32.33 | reduce-window | flops 4161536 | bytes 262148 | tf_op jit(solution)/shard_map/reduce-window.8
  1055.3 5.6 slice_bitcast_fusion.1
  1076.2 5.9 fusion.105
  1083.3 11.9 fusion.110
  1097.2 9.8 fusion.174
  1112.3 6.3 collective-permute-done.3
  1120.0 12.9 fusion.104
  1133.0 6.3 fusion.124
  1139.4 9.0 convolution_add_fusion.2
  1148.4 6.5 convert_element_type.109
  1154.9 72.6 %all-reduce.21.cloned.1.call-done = (f32[8,1024,16]{1,0,2:T(8,128)}, f32[8,16,1024]{2,0,1:T(8,128)}) async-done(((f32[8,1024,16]{1,0,2:T(8,128)}, f32[8,16,1024]{2,0,1:T(8,128)}), (f32[8,1024,16]{1,0,2:T(8,128)}, f32[8,16,1024]{2,0,1:T(8,128)})) %all-reduce.21.cloned.1.call-update) | async-done | bytes 1048592 | tf_op jit(solution)/shard_map/psum | solution.py:301
  1231.8 118.2 %all-reduce.23.cloned.1.call-done = (f32[8,16,2,1024]{3,0,2,1:T(8,128)}, f32[8,1024,16]{1,0,2:T(8,128)}) async-done(((f32[8,16,2,1024]{3,0,2,1:T(8,128)}, f32[8,1024,16]{1,0,2:T(8,128)}), (f32[8,16,2,1024]{3,0,2,1:T(8,128)}, f32[8,1024,16]{1,0,2:T(8,128)})) %all-reduce.23.cloned.1.call-update) | async-done | bytes 1572880 | tf_op jit(solution)/shard_map/psum | solution.py:300
  1355.1 34.2 %all-reduce.19.cloned.1.call-done = f32[2,1024,1024]{2,1,0:T(8,128)} async-done(((f32[2,1024,1024]{2,1,0:T(8,128)}), f32[2,1024,1024]{2,1,0:T(8,128)}) %all-reduce.19.cloned.1.call-update) | async-done | bytes 8388624 | tf_op jit(solution)/shard_map/psum | solution.py:286
  1389.3 9.0 multiply_reduce_fusion.4
  1398.3 10.7 reduce-scatter.3.cloned.1.call-done
  1409.1 8.1 fusion.109
  (572 shorter events, 501.5 us)
Async XLA Ops:
  7.2 147.1 %copy-start = (bf16[1024,1024]{1,0:T(8,128)(2,1)S(1)}, bf16[1024,1024]{1,0:T(8,128)(2,1)}, u32[]{:S(2)}) copy-start(bf16[1024,1024]{1,0:T(8,128)(2,1)} %param.43) | copy-start | bytes 6291460
  7.2 119.2 %all-gather.7.cloned.1.call-start = ((), (), s32[]{:S(2)}) async-start(), calls=%async_computation.2 | async-start | bytes 1572864 | tf_op jit(solution)/shard_map/all_gather | solution.py:175
  11.0 55.4 %copy-start.54 = (f32[2,1024]{1,0:T(2,128)}, f32[2,1024]{1,0:T(2,128)S(1)}, u32[]{:S(2)}) copy-start(f32[2,1024]{1,0:T(2,128)S(1)} %get-tuple-element.1042) | copy-start | bytes 24580
  19.2 16.0 %copy-start.7 = (bf16[2,1024,1024]{2,1,0:T(8,128)(2,1)S(1)}, bf16[2,1024,1024]{2,1,0:T(8,128)(2,1)}, u32[]{:S(2)}) copy-start(bf16[2,1024,1024]{2,1,0:T(8,128)(2,1)} %param.30) | copy-start | bytes 12582916
  19.2 16.0 %copy-start.73 = (f32[1024]{0:T(1024)S(1)}, f32[1024]{0:T(1024)}, u32[]{:S(2)}) copy-start(f32[1024]{0:T(1024)} %param.33) | copy-start | bytes 12292
  51.1 15.3 %copy-start.51 = (bf16[1024,16]{0,1:T(8,128)(2,1)S(1)}, bf16[1024,16]{0,1:T(8,128)(2,1)}, u32[]{:S(2)}) copy-start(bf16[1024,16]{0,1:T(8,128)(2,1)} %param.36) | copy-start | bytes 98308
  55.9 39.8 %collective-permute-start = (bf16[2,3,1024]{2,1,0:T(4,128)(2,1)S(1)}, bf16[2,3,1024]{2,1,0:T(4,128)(2,1)S(1)}, u32[]{:S(2)}, u32[]{:S(2)}) collective-permute-start(bf16[2,3,1024]{2,1,0:T(4,128)(2,1)S(1)} %slice.280), channel_id=1, source_target_pairs={{0,8},{8,16},{16,24},{1,9},{9,17},{17,25},{2,10},{10,18},{18,26},{... | collective-permute-start | bytes 36872 | tf_op jit(solution)/shard_map/ppermute | solution.py:16
  62.5 24.6 %copy-start.60 = (f32[5,1024]{1,0:T(8,128)S(1)}, f32[5,1024]{1,0:T(8,128)}, u32[]{:S(2)}) copy-start(f32[5,1024]{1,0:T(8,128)} %param.37) | copy-start | bytes 61444
  62.6 27.8 %copy-start.66 = (f32[5,2,64]{2,1,0:T(2,128)S(1)}, f32[5,2,64]{2,1,0:T(2,128)}, u32[]{:S(2)}) copy-start(f32[5,2,64]{2,1,0:T(2,128)} %param.38) | copy-start | bytes 7684
  62.6 29.3 %collective-permute-start.1 = (bf16[2,3,2,64]{1,3,2,0:T(8,128)(2,1)S(1)}, bf16[2,3,2,64]{1,3,2,0:T(8,128)(2,1)S(1)}, u32[]{:S(2)}, u32[]{:S(2)}) collective-permute-start(bf16[2,3,2,64]{1,3,2,0:T(8,128)(2,1)S(1)} %slice.285), channel_id=1, source_target_pairs={{0,8},{8,16},{16,24},{1,9},{9,17},{17,25},{2,10},{10,18},{18,26},{... | collective-permute-start | bytes 4616 | tf_op jit(solution)/shard_map/ppermute | solution.py:16
  68.1 18.4 %copy-start.13 = (bf16[2,1024,16]{2,0,1:T(2,128)(2,1)}, bf16[2,1024,16]{2,0,1:T(2,128)(2,1)S(1)}, u32[]{:S(2)}) copy-start(bf16[2,1024,16]{2,0,1:T(2,128)(2,1)S(1)} %copy.358) | copy-start | bytes 196612
  68.2 19.0 %copy-start.71 = (f32[16]{0:T(128)}, f32[16]{0:T(128)S(1)}, u32[]{:S(2)}) copy-start(f32[16]{0:T(128)S(1)} %exponential_negate_fusion) | copy-start | bytes 196
  87.1 15.3 %copy-start.11 = (f32[2,16,8,128]{1,0,3,2:T(2,128)}, f32[2,16,8,128]{1,0,3,2:T(2,128)S(1)}, u32[]{:S(2)}) copy-start(f32[2,16,8,128]{1,0,3,2:T(2,128)S(1)} %copy.362) | copy-start | bytes 393220
  87.2 15.2 %copy-start.43 = (f32[1,1024]{1,0:T(1,128)}, f32[1,1024]{1,0:T(1,128)S(1)}, u32[]{:S(2)}) copy-start(f32[1,1024]{1,0:T(1,128)S(1)} %get-tuple-element.1037) | copy-start | bytes 12292
  87.2 15.2 %copy-start.45 = (f32[1,1024]{1,0:T(1,128)}, f32[1,1024]{1,0:T(1,128)S(1)}, u32[]{:S(2)}) copy-start(f32[1,1024]{1,0:T(1,128)S(1)} %get-tuple-element.1039) | copy-start | bytes 12292
  87.2 15.2 %copy-start.47 = (f32[1,1024]{1,0:T(1,128)}, f32[1,1024]{1,0:T(1,128)S(1)}, u32[]{:S(2)}) copy-start(f32[1,1024]{1,0:T(1,128)S(1)} %get-tuple-element.1040) | copy-start | bytes 12292
  87.2 15.2 %copy-start.49 = (f32[1,1024]{1,0:T(1,128)}, f32[1,1024]{1,0:T(1,128)S(1)}, u32[]{:S(2)}) copy-start(f32[1,1024]{1,0:T(1,128)S(1)} %get-tuple-element.1038) | copy-start | bytes 12292
  91.9 34.5 %copy-start.23 = (f32[2,1024,16]{1,2,0:T(8,128)}, f32[2,1024,16]{1,2,0:T(8,128)S(1)}, u32[]{:S(2)}) copy-start(f32[2,1024,16]{1,2,0:T(8,128)S(1)} %copy.364) | copy-start | bytes 393220
  95.4 119.2 %all-gather.9.cloned.1.call-start = ((), (), s32[]{:S(2)}) async-start(), calls=%async_computation.6 | async-start | bytes 5242880 | tf_op jit(solution)/shard_map/all_gather | solution.py:21
  120.1 17.3 %copy-start.67 = (f32[16]{0:T(128)S(1)}, f32[16]{0:T(128)}, u32[]{:S(2)}) copy-start(f32[16]{0:T(128)} %param.41) | copy-start | bytes 196
  120.1 26.9 %copy-start.56 = (s32[2]{0:T(128)S(1)}, s32[2]{0:T(128)}, u32[]{:S(2)}) copy-start(s32[2]{0:T(128)} %param.32) | copy-start | bytes 28
  133.9 789.7 %all-gather.11.cloned.1.call-start = ((), (), s32[]{:S(2)}) async-start(), calls=%async_computation.7 | async-start | bytes 5242880 | tf_op jit(solution)/shard_map/all_gather | solution.py:21
  154.2 197.9 %copy-start.30 = (f32[2,16,1024]{2,1,0:T(8,128)}, f32[2,16,1024]{2,1,0:T(8,128)S(1)}, u32[]{:S(2)}) copy-start(f32[2,16,1024]{2,1,0:T(8,128)S(1)} %fusion.179) | copy-start | bytes 393220
  337.6 14.5 %copy-start.40 = (f32[2,1024,16]{1,0,2:T(2,128)S(1)}, f32[2,1024,16]{1,0,2:T(2,128)}, u32[]{:S(2)}) copy-start(f32[2,1024,16]{1,0,2:T(2,128)} %get-tuple-element.1058) | copy-start | bytes 393220
  337.6 14.5 %copy-start.76 = (f32[1024]{0:T(1024)S(1)}, f32[1024]{0:T(1024)}, u32[]{:S(2)}) copy-start(f32[1024]{0:T(1024)} %param.42) | copy-start | bytes 12292
  422.3 422.0 %copy-start.42 = (f32[4,2,16]{2,1,0:T(2,128)S(1)}, f32[4,2,16]{2,1,0:T(2,128)}, u32[]{:S(2)}) copy-start(f32[4,2,16]{2,1,0:T(2,128)} %copy-done.41) | copy-start | bytes 1540
  453.9 14.0 copy-start.4
  475.1 18.7 %copy-start.25 = (f32[2,256,16]{1,2,0:T(8,128)}, f32[2,256,16]{1,2,0:T(8,128)S(1)}, u32[]{:S(2)}) copy-start(f32[2,256,16]{1,2,0:T(8,128)S(1)} %copy.570) | copy-start | bytes 98308 | tf_op jit(solution)/shard_map/transpose(jvp())/while
  478.6 15.3 %copy-start.26 = (f32[2,256,16]{1,2,0:T(8,128)}, f32[2,256,16]{1,2,0:T(8,128)S(1)}, u32[]{:S(2)}) copy-start(f32[2,256,16]{1,2,0:T(8,128)S(1)} %copy.568) | copy-start | bytes 98308 | tf_op jit(solution)/shard_map/transpose(jvp())/while
  493.9 35.0 %copy-start.22 = (pred[1,256,256,1]{2,1,3,0:T(8,128)(4,1)S(1)}, pred[1,256,256,1]{2,1,3,0:T(8,128)(4,1)}, u32[]{:S(2)}) copy-start(pred[1,256,256,1]{2,1,3,0:T(8,128)(4,1)} %iota_compare_fusion.12) | copy-start | bytes 196612 | tf_op jit(solution)/shard_map/transpose(jvp())/while
  525.8 13.0 copy-start.1
  553.4 15.2 %copy-start.4 = (f32[2,256,128]{2,1,0:T(8,128)}, f32[2,256,128]{2,1,0:T(8,128)S(1)}, u32[]{:S(2)}) copy-start(f32[2,256,128]{2,1,0:T(8,128)S(1)} %get-tuple-element.1302) | copy-start | bytes 786436 | tf_op jit(solution)/shard_map/transpose(jvp())/while
  575.9 18.7 %copy-start.25 = (f32[2,256,16]{1,2,0:T(8,128)}, f32[2,256,16]{1,2,0:T(8,128)S(1)}, u32[]{:S(2)}) copy-start(f32[2,256,16]{1,2,0:T(8,128)S(1)} %copy.570) | copy-start | bytes 98308 | tf_op jit(solution)/shard_map/transpose(jvp())/while
  579.3 15.3 %copy-start.26 = (f32[2,256,16]{1,2,0:T(8,128)}, f32[2,256,16]{1,2,0:T(8,128)S(1)}, u32[]{:S(2)}) copy-start(f32[2,256,16]{1,2,0:T(8,128)S(1)} %copy.568) | copy-start | bytes 98308 | tf_op jit(solution)/shard_map/transpose(jvp())/while
  594.6 35.0 %copy-start.22 = (pred[1,256,256,1]{2,1,3,0:T(8,128)(4,1)S(1)}, pred[1,256,256,1]{2,1,3,0:T(8,128)(4,1)}, u32[]{:S(2)}) copy-start(pred[1,256,256,1]{2,1,3,0:T(8,128)(4,1)} %iota_compare_fusion.12) | copy-start | bytes 196612 | tf_op jit(solution)/shard_map/transpose(jvp())/while
  654.1 15.2 %copy-start.4 = (f32[2,256,128]{2,1,0:T(8,128)}, f32[2,256,128]{2,1,0:T(8,128)S(1)}, u32[]{:S(2)}) copy-start(f32[2,256,128]{2,1,0:T(8,128)S(1)} %get-tuple-element.1302) | copy-start | bytes 786436 | tf_op jit(solution)/shard_map/transpose(jvp())/while
  676.6 18.7 %copy-start.25 = (f32[2,256,16]{1,2,0:T(8,128)}, f32[2,256,16]{1,2,0:T(8,128)S(1)}, u32[]{:S(2)}) copy-start(f32[2,256,16]{1,2,0:T(8,128)S(1)} %copy.570) | copy-start | bytes 98308 | tf_op jit(solution)/shard_map/transpose(jvp())/while
  680.0 15.3 %copy-start.26 = (f32[2,256,16]{1,2,0:T(8,128)}, f32[2,256,16]{1,2,0:T(8,128)S(1)}, u32[]{:S(2)}) copy-start(f32[2,256,16]{1,2,0:T(8,128)S(1)} %copy.568) | copy-start | bytes 98308 | tf_op jit(solution)/shard_map/transpose(jvp())/while
  695.3 34.9 %copy-start.22 = (pred[1,256,256,1]{2,1,3,0:T(8,128)(4,1)S(1)}, pred[1,256,256,1]{2,1,3,0:T(8,128)(4,1)}, u32[]{:S(2)}) copy-start(pred[1,256,256,1]{2,1,3,0:T(8,128)(4,1)} %iota_compare_fusion.12) | copy-start | bytes 196612 | tf_op jit(solution)/shard_map/transpose(jvp())/while
  754.7 15.2 %copy-start.4 = (f32[2,256,128]{2,1,0:T(8,128)}, f32[2,256,128]{2,1,0:T(8,128)S(1)}, u32[]{:S(2)}) copy-start(f32[2,256,128]{2,1,0:T(8,128)S(1)} %get-tuple-element.1302) | copy-start | bytes 786436 | tf_op jit(solution)/shard_map/transpose(jvp())/while
  777.2 18.7 %copy-start.25 = (f32[2,256,16]{1,2,0:T(8,128)}, f32[2,256,16]{1,2,0:T(8,128)S(1)}, u32[]{:S(2)}) copy-start(f32[2,256,16]{1,2,0:T(8,128)S(1)} %copy.570) | copy-start | bytes 98308 | tf_op jit(solution)/shard_map/transpose(jvp())/while
  780.7 15.3 %copy-start.26 = (f32[2,256,16]{1,2,0:T(8,128)}, f32[2,256,16]{1,2,0:T(8,128)S(1)}, u32[]{:S(2)}) copy-start(f32[2,256,16]{1,2,0:T(8,128)S(1)} %copy.568) | copy-start | bytes 98308 | tf_op jit(solution)/shard_map/transpose(jvp())/while
  795.9 35.0 %copy-start.22 = (pred[1,256,256,1]{2,1,3,0:T(8,128)(4,1)S(1)}, pred[1,256,256,1]{2,1,3,0:T(8,128)(4,1)}, u32[]{:S(2)}) copy-start(pred[1,256,256,1]{2,1,3,0:T(8,128)(4,1)} %iota_compare_fusion.12) | copy-start | bytes 196612 | tf_op jit(solution)/shard_map/transpose(jvp())/while
  844.2 262.8 %reduce-scatter.5.cloned.1.call-start = ((), (), s32[]{:S(2)}) async-start(), calls=%async_computation.4 | async-start | bytes 3145728 | tf_op jit(solution)/shard_map/reduce_scatter | solution.py:243
  852.6 16.2 %copy-start.57 = (s32[2]{0:T(128)S(1)}, s32[2]{0:T(128)}, u32[]{:S(2)}) copy-start(s32[2]{0:T(128)} %param.32) | copy-start | bytes 28
  852.6 17.5 %copy-start.35 = (bf16[2,1024,16]{1,0,2:T(2,128)(2,1)S(1)}, bf16[2,1024,16]{1,0,2:T(2,128)(2,1)}, u32[]{:S(2)}) copy-start(bf16[2,1024,16]{1,0,2:T(2,128)(2,1)} %get-tuple-element.1057) | copy-start | bytes 196612
  963.2 15.1 %copy-start.3 = (f32[2,1024,1024]{2,1,0:T(8,128)}, f32[2,1024,1024]{2,1,0:T(8,128)S(1)}, u32[]{:S(2)}) copy-start(f32[2,1024,1024]{2,1,0:T(8,128)S(1)} %get-tuple-element.998) | copy-start | bytes 25165828
  978.3 13.1 copy-start.6
  978.3 14.8 %copy-start.14 = (f32[2,1024,128]{1,2,0:T(8,128)S(1)}, f32[2,1024,128]{1,2,0:T(8,128)}, u32[]{:S(2)}) copy-start(f32[2,1024,128]{1,2,0:T(8,128)} %reshape.375) | copy-start | bytes 3145732
  991.7 73.7 %collective-permute-start.2 = (f32[2,3,1024]{2,1,0:T(4,128)S(1)}, f32[2,3,1024]{2,1,0:T(4,128)S(1)}, u32[]{:S(2)}, u32[]{:S(2)}) collective-permute-start(f32[2,3,1024]{2,1,0:T(4,128)S(1)} %pad_add_fusion.4), channel_id=1, source_target_pairs={{8,0},{16,8},{24,16},{9,1},{17,9},{25,17},{10,2},{18,10},{26,18},{... | collective-permute-start | bytes 73736 | tf_op jit(solution)/shard_map/ppermute | solution.py:16
  1000.4 50.9 %copy-start.12 = (f32[2,16,8,128]{1,0,3,2:T(2,128)S(1)}, f32[2,16,8,128]{1,0,3,2:T(2,128)}, u32[]{:S(2)}) copy-start(f32[2,16,8,128]{1,0,3,2:T(2,128)} %copy-done.11) | copy-start | bytes 393220
  1000.4 50.9 %copy-start.70 = (f32[16]{0:T(128)S(1)}, f32[16]{0:T(128)}, u32[]{:S(2)}) copy-start(f32[16]{0:T(128)} %param.39) | copy-start | bytes 196
  1000.4 50.9 %copy-start.72 = (f32[16]{0:T(128)S(1)}, f32[16]{0:T(128)}, u32[]{:S(2)}) copy-start(f32[16]{0:T(128)} %copy-done.71) | copy-start | bytes 196
  1001.9 225.6 %all-reduce.21.cloned.1.call-start = ((), (), s32[]{:S(2)}) async-start(), calls=%async_computation.8 | async-start | bytes 2097152 | tf_op jit(solution)/shard_map/psum | solution.py:301
  1009.9 51.0 %copy-start.52 = (bf16[1024,16]{0,1:T(8,128)(2,1)S(1)}, bf16[1024,16]{0,1:T(8,128)(2,1)}, u32[]{:S(2)}) copy-start(bf16[1024,16]{0,1:T(8,128)(2,1)} %param.36) | copy-start | bytes 98308
  1051.3 14.1 slice-start.2
  1083.3 13.8 copy-start.28
  1095.2 13.4 copy-start.62
  1095.3 254.7 %all-reduce.23.cloned.1.call-start = ((), (), s32[]{:S(2)}) async-start(), calls=%async_computation.9 | async-start | bytes 3145728 | tf_op jit(solution)/shard_map/psum | solution.py:300
  1106.9 282.3 %all-reduce.19.cloned.1.call-start = ((), (), s32[]{:S(2)}) async-start(), calls=%async_computation.5 | async-start | bytes 16777216 | tf_op jit(solution)/shard_map/psum | solution.py:286
  1109.8 8.8 collective-permute-start.3
  1133.0 276.1 %reduce-scatter.3.cloned.1.call-start = ((), (), s32[]{:S(2)}) async-start(), calls=%async_computation.3 | async-start | bytes 12582912 | tf_op jit(solution)/shard_map/reduce_scatter | solution.py:208
  1148.4 240.9 %copy-start.75 = (f32[1024]{0:T(1024)S(1)}, f32[1024]{0:T(1024)}, u32[]{:S(2)}) copy-start(f32[1024]{0:T(1024)} %param.33) | copy-start | bytes 12292
  1355.1 53.9 %copy-start.53 = (f32[2,1024]{1,0:T(2,128)S(1)}, f32[2,1024]{1,0:T(2,128)}, u32[]{:S(2)}) copy-start(f32[2,1024]{1,0:T(2,128)} %get-tuple-element.1041) | copy-start | bytes 24580
  (49 other events, 409.0 us)
Sparse Core Ops, SparseCore 0:
  95.5 8.2 all-gather.6
  134.0 80.5 all-gather.8
  844.4 79.2 all-gather.10
  1002.0 10.2 reduce-scatter.4
  1095.4 132.0 all-reduce.20
  1233.3 116.6 all-reduce.22
  1352.4 36.8 all-reduce.18
  1391.6 17.4 reduce-scatter.2
where the time goes:
time: 1440 us; the launch traced here: 1420 us
  matrix products  490 us (34%)
  waiting for transfers between devices  302 us (21%)
  local copies, waits for them, and re-layouts  297 us (21%)
  other arithmetic  273 us (19%)
  loops' own time  21.6 us (2%)
  between operations  15.4 us (1%)
    dot_general x12, matrix products, one_block(): jnp.einsum('stuh,suhp->sthp', weights, x_block, precision=EXACT_MATMUL)  145 us
    psum x1, waiting for transfers between devices, local(): lax.psum((local_sums[0], local_sums[1]), ('seq', 'batch'))  118 us
    another operation x38, other arithmetic  79.1 us
    psum x1, waiting for transfers between devices, local(): lax.psum((shared_sums[0], shared_sums[1]), ('seq', 'head', 'batch'))  72.6 us
    dot_general x16, matrix products, one_block(): jnp.einsum('stn,shpn->sthp', c_block, carry_state, precision=EXACT_MATMUL)  65.6 us
    all_gather x2, waiting for transfers between devices, entering(): pieces = jax.tree.map(lambda part: lax.all_gather(part, axis), value)  60.1 us
    dot_general x12, matrix products, one_block(): jnp.einsum('suh,suhp,sun->shpn', tail_weight, x_block, b_block, precision...  54.5 us
    squeeze x20, local copies, waits for them, and re-layouts, local_scan(): _, scanned = lax.scan(jax.checkpoint(one_block), incoming, pieces)  43 us
  transfers between devices with their start and end apart: 12, of which 7 were waited for; matrix products, arithmetic and copies ran while one was open for 23% of the time, Pallas kernels for 0%

commit v1 on v0

v1 whole, which is shorter than its diff:
```python
import functools

import jax
import jax.numpy as jnp
from jax import lax
from jax.experimental import pallas as pl
from jax.experimental.pallas import tpu as pltpu
from jax.sharding import PartitionSpec as P

EPSILON = 1e-05
LOG2E = 1.4426950408889634
CHUNK = 128
LANES = 128
HALO = 16
BF = jnp.bfloat16
F32 = jnp.float32
VMEM_LIMIT = 60 * 1024 * 1024


def mm(a, b):
    return lax.dot_general(a, b, (((1,), (0,)), ((), ())), preferred_element_type=F32)


def nt(a, b):
    return lax.dot_general(a, b, (((1,), (1,)), ((), ())), preferred_element_type=F32)


def tn(a, b):
    return lax.dot_general(a, b, (((0,), (0,)), ((), ())), preferred_element_type=F32)


def lane_of(shape):
    return lax.broadcasted_iota(jnp.int32, shape, len(shape) - 1)


def row_of(shape):
    return lax.broadcasted_iota(jnp.int32, shape, len(shape) - 2)


def split_dup(v, rank):
    high = v.astype(BF)
    rest = (v - high.astype(F32)).astype(BF)
    return jnp.where(lane_of(v.shape) < rank, high, rest)


def fold(v, rank):
    return v[:rank] + v[rank : 2 * rank]


def expand(v, spread):
    high = v.astype(BF)
    rest = (v - high.astype(F32)).astype(BF)
    return mm(jnp.concatenate([high, rest], 1), spread)


def parts(v):
    high = v.astype(BF)
    return high, (v - high.astype(F32)).astype(BF)


def gather(v, emap):
    high, rest = parts(v)
    return nt(high, emap) + nt(rest, emap)


def both(product, a, b):
    if not isinstance(a, tuple):
        return product(a, b[0]) + product(a, b[1])
    if not isinstance(b, tuple):
        return product(a[0], b) + product(a[1], b)
    return product(a[0], b[0]) + product(a[0], b[1]) + product(a[1], b[0])


def paired(ws):
    return tuple(jnp.concatenate([ws[0][i], ws[1][i]], 1) for i in range(2))


def tri_sum(tri, v):
    a = v.astype(BF)
    r = v - a.astype(F32)
    b = r.astype(BF)
    c = (r - b.astype(F32)).astype(BF)
    w = v.shape[1]
    out = mm(tri, jnp.concatenate([a, b, c], 1))
    return out[:, :w] + out[:, w : 2 * w] + out[:, 2 * w :]


def sigm(v):
    return 0.5 * jnp.tanh(0.5 * v) + 0.5


def softplus(v):
    return jnp.maximum(v, 0.0) + jnp.log(1.0 + jnp.exp(-jnp.abs(v)))


def params(n):
    return pltpu.CompilerParams(
        dimension_semantics=("arbitrary",) * n, vmem_limit_bytes=VMEM_LIMIT
    )


def halves(v, h):
    w = v.shape[1] // 2
    lo, hi = v[:, :w], v[:, w:]
    return jnp.where(h == 0, lo, hi), jnp.where(h == 0, hi, lo)


def unweave_kernel(w, even, odd):
    n = w.shape[0]
    r = row_of((n, n))
    c = lane_of((n, n))
    m = (c == jnp.where(r < n // 2, 2 * r, 2 * r - n + 1)).astype(BF)
    out = mm(m, w[...]).astype(BF)
    even[...] = out[: n // 2]
    odd[...] = out[n // 2 :]


def front_kernel(
    tok, prev, halo, gain, wz, wx, wbc, wst, dn, upz, upx, cvx, cvb,
    z, xc, slx, bcc, slb, dtr, lrh, xs, bs, *, rank,
):
    t = pl.program_id(1)
    rows = tok.shape[1]

    def normed(v):
        f = v.astype(F32)
        scale = lax.rsqrt(jnp.mean(f * f, -1, keepdims=True) + EPSILON)
        return (f * scale * gain[...]).astype(BF)

    before = jnp.where(t == 0, halo[0], prev[0])
    ext = jnp.concatenate([normed(before), normed(tok[0])], 0)
    main = ext[HALO:]
    low = split_dup(nt(ext, dn[0]), rank)
    lrh[0] = low[HALO:]
    z[0] = (mm(main, wz[...]) + mm(low[HALO:], upz[0])).astype(BF)
    dtr[0] = mm(main, wst[...]).astype(BF).astype(F32)

    def conv(raw, keep, taps, act, slope):
        keep[...] = raw.astype(BF).astype(F32)
        pre = taps[4:5]
        for k in range(4):
            pre = pre + taps[k : k + 1] * keep[HALO - 3 + k : HALO - 3 + k + rows]
        s = sigm(pre)
        a = pre * s
        act[0] = a.astype(BF)
        slope[0] = s + a * (1.0 - s)

    conv(mm(ext, wx[...]) + mm(low, upx[0]), xs, cvx[...], xc, slx)
    conv(mm(ext, wbc[...]), bs, cvb[...], bcc, slb)


def state_kernel(dtr, xc, bcc, bias, na, spread, cum, vv, rc, cumT, vT, rs, sc, send, st, run):
    c = pl.program_id(1)
    q = CHUNK
    n = bcc.shape[2] // 2

    @pl.when(c == 0)
    def _():
        st[...] = jnp.zeros_like(st)
        run[...] = jnp.zeros_like(run)

    dt = softplus(dtr[0] + bias[...])
    tri = (row_of((q, q)) >= lane_of((q, q))).astype(BF)
    cm = tri_sum(tri, dt * na[...])
    v = cm - jnp.log2(dt)
    cum[0] = cm
    vv[0] = v
    rc[0] = cm + run[0:1]
    hr = cumT.shape[1]
    cumT[0] = jnp.transpose(cm)[:hr]
    vT[0] = jnp.transpose(v)[:hr]
    rs[0, 0] = run[...]
    sc[0, 0] = st[...]
    last = cm[q - 1 : q]
    w = expand(jnp.exp2(last - v), spread[...])
    wx = parts(w * xc[0].astype(F32))
    dec = expand(jnp.exp2(jnp.broadcast_to(last, (8, LANES))), spread[...])[0:1]
    st[...] = dec * st[...] + both(tn, bcc[0][:, :n], wx)
    run[...] = run[...] + last

    @pl.when(c == pl.num_programs(1) - 1)
    def _():
        send[0, :n] = st[...].astype(BF)
        total = expand(jnp.exp2(run[...]), spread[...])
        high = total.astype(BF)
        rest = (total - high.astype(F32)).astype(BF)
        send[0, n:] = jnp.concatenate([high, rest], 0)


def intra_kernel(xc, bcc, cum, vT, sc, skip, spread, y, *, heads):
    q = CHUNK
    n = bcc.shape[2] // 2
    b = bcc[0][:, :n]
    c = bcc[0][:, n:]
    scores = nt(c, b)
    allowed = row_of((q, q)) >= lane_of((q, q))
    cm = cum[0]
    e = expand(jnp.exp2(cm), spread[...])
    y[0] = both(mm, c, parts(sc[0, 0])) * e + skip[...] * xc[0].astype(F32)
    first = lane_of((q, LANES)) < LANES // 2
    for j in range(heads // 2):
        ws = []
        for h in (2 * j, 2 * j + 1):
            d = cm[:, h : h + 1] - vT[0, h : h + 1, :]
            ws.append(parts(jnp.exp2(jnp.where(allowed, d, -jnp.inf)) * scores))
        cols = slice(j * LANES, (j + 1) * LANES)
        xp = xc[0, :, cols]
        zero = jnp.zeros_like(xp)
        xbd = jnp.concatenate([jnp.where(first, xp, zero), jnp.where(first, zero, xp)], 0)
        y[0, :, cols] += both(mm, paired(ws), xbd)


def dnormout_kernel(g, wo, od, ou, dno, blh, *, rank):
    low = split_dup(nt(g[0], ou[0]), rank)
    blh[0] = low
    dno[0] = nt(g[0], wo[...]) + mm(low, od[0])


def gated_of(yl, bcc, rc, sin, z, spread):
    n = bcc.shape[2] // 2
    y = yl[0] + expand(jnp.exp2(rc[0]), spread[...]) * both(mm, bcc[0][:, n:], parts(sin[0]))
    gate = z[0].astype(F32)
    s = sigm(gate)
    return y, gate, s


def sums_kernel(yl, bcc, rc, sin, z, dno, og, spread, sums):
    y, gate, s = gated_of(yl, bcc, rc, sin, z, spread)
    gated = y * (gate * s)
    sq = jnp.sum(gated * gated, -1, keepdims=True)
    tot = jnp.sum(dno[0] * og[...] * gated, -1, keepdims=True)
    sums[0] = jnp.where(lane_of(sums.shape[1:]) == 0, sq, tot)


def gate_back_kernel(
    yl, bcc, rc, cum, sin, z, dno, sums, og, spread, no, dzr, dy, dc, send, dst, *, full
):
    step = pl.program_id(1)
    q = CHUNK
    n = bcc.shape[2] // 2

    @pl.when(step == 0)
    def _():
        dst[...] = jnp.zeros_like(dst)

    y, gate, s = gated_of(yl, bcc, rc, sin, z, spread)
    act = gate * s
    gated = y * act
    r = lax.rsqrt(sums[0][:, 0:1] / full + EPSILON)
    k = r * r * r * (sums[0][:, 1:2] / full)
    no[0] = (gated * r * og[...]).astype(BF)
    dg = r * (og[...] * dno[0]) - gated * k
    dzr[0] = (dg * y * (s + act * (1.0 - s))).astype(BF)
    dyv = dg * act
    dy[0] = dyv
    dc[0, 0] = dst[...]
    e = expand(jnp.exp2(cum[0]), spread[...])
    dst[...] = e[q - 1 : q] * dst[...] + both(tn, bcc[0][:, n:], parts(e * dyv))

    @pl.when(step == pl.num_programs(1) - 1)
    def _():
        send[0] = dst[...].astype(BF)


def out_kernel(head, no, g, tok, wo, od, ou, blh, keep, send, god, gou, *, rank):
    t = pl.program_id(1)

    @pl.when(t == 0)
    def _():
        god[...] = jnp.zeros_like(god)
        gou[...] = jnp.zeros_like(gou)

    low = split_dup(nt(no[0], od[0]), rank)
    own, other = halves(mm(no[0], wo[...]) + mm(low, ou[0]), head[0])
    keep[0] = own + halves(tok[0].astype(F32), head[0])[0]
    send[0] = other.astype(BF)
    god[0] += fold(tn(blh[0], no[0]), rank)
    gou[0] += fold(tn(low, g[0]), rank)


def scan_back_kernel(
    xc, bcc, dy, cumT, cum, vv, rc, rs, sc, sin, dc, dret, total, dtr, bias, na, skip, slx, slb,
    emap, spread, dpx, dpb, ddt, rowq, *, heads,
):
    q = CHUNK
    n = bcc.shape[2] // 2
    b = bcc[0][:, :n]
    c = bcc[0][:, n:]
    sT = nt(b, c)
    allowed = lane_of((q, q)) >= row_of((q, q))
    sT = jnp.where(allowed, sT, 0.0)
    cm = cum[0]
    v = vv[0]
    last = cm[q - 1 : q]
    first = lane_of((q, LANES)) < LANES // 2
    lanes = lane_of((q, LANES))
    rowq[...] = jnp.zeros_like(rowq)
    ds = jnp.zeros((q, q), F32)
    colq = jnp.zeros((q, LANES), F32)
    head8 = jnp.concatenate(
        [rs[0, 0][0:1], total[0][0:1] - rc[0][q - 1 : q], last, jnp.zeros((5, LANES), F32)], 0
    )
    decs = expand(jnp.exp2(head8), spread[...])
    s_in = sc[0, 0] + decs[0:1] * sin[0]
    d_out = dc[0, 0] + decs[1:2] * dret[0]
    s_two = parts(s_in)
    d_two = parts(d_out)
    x = xc[0].astype(F32)
    dyf = dy[0]
    e = expand(jnp.exp2(cm), spread[...])
    w = expand(jnp.exp2(last - v), spread[...])
    ed = e * dyf
    carried = both(mm, c, s_two)
    wbd = w * both(mm, b, d_two)
    wx = w * x
    up = gather(ed * carried, emap[...])
    vs = gather(x * wbd, emap[...])
    cross = gather(d_out * s_in, emap[...])
    crossed = jnp.sum(cross, 0, keepdims=True) * jnp.exp2(last)
    d_c = both(nt, parts(ed), s_two)
    d_b = both(nt, parts(wx), d_two)
    slope = slx[0]
    base = wbd + skip[...] * dyf
    for j in range(heads // 2):
        cols = slice(j * LANES, (j + 1) * LANES)
        xp = xc[0, :, cols]
        dbd = []
        for dp in parts(dyf[:, cols]):
            zero = jnp.zeros_like(dp)
            dbd.append(jnp.concatenate([jnp.where(first, dp, zero), jnp.where(first, zero, dp)], 0))
        dbd = tuple(dbd)
        dw = both(nt, xp, dbd)
        ws = []
        for i, h in enumerate((2 * j, 2 * j + 1)):
            d = cumT[0, h : h + 1, :] - v[:, h : h + 1]
            ex = jnp.exp2(jnp.where(allowed, d, -jnp.inf))
            ws.append(parts(ex * sT))
            dwe = dw[:, i * q : (i + 1) * q] * ex
            ds = ds + dwe
            qm = dwe * sT
            rowq[h : h + 1, :] = jnp.sum(qm, 0, keepdims=True)
            colq = jnp.where(lanes == h, jnp.sum(qm, 1, keepdims=True), colq)
        dx = both(mm, paired(ws), dbd) + base[:, cols]
        dpx[0, :, cols] = dx * slope[:, cols]
    ds_two = parts(ds)
    d_b = d_b + both(mm, ds_two, c)
    d_c = d_c + both(tn, ds_two, b)
    dpb[0] = jnp.concatenate([d_b, d_c], 1) * slb[0]
    rq = jnp.transpose(rowq[...])
    upper = (row_of((q, q)) <= lane_of((q, q))).astype(BF)
    lower = (row_of((q, q)) > lane_of((q, q))).astype(BF)
    dlog = tri_sum(upper, rq - colq + up) + tri_sum(lower, vs) + crossed
    raw = dtr[0] + bias[...]
    dt = softplus(raw)
    sg = jax.nn.sigmoid(raw)
    ratio = sg / jnp.maximum(dt, 1e-37)
    out = (colq + vs) * ratio + dlog * (na[...] * (1.0 / LOG2E)) * sg
    ddt[0] = jnp.where(lanes < heads, out, 0.0).astype(BF)


def back_kernel(
    head, dpx, nxx, hax, dpb, nxb, hab, dzr, ddt, tok, cot, gain, lrh, wz, wx, wbc, wst, dn, upz, upx, cvx, cvb,
    kept, send, giz, gix, gid, xs, bs, *, rank,
):
    t = pl.program_id(1)
    rows = tok.shape[1]
    end = t == pl.num_programs(1) - 1

    @pl.when(t == 0)
    def _():
        giz[...] = jnp.zeros_like(giz)
        gix[...] = jnp.zeros_like(gix)
        gid[...] = jnp.zeros_like(gid)

    def conv(tile, nxt, halo, keep, taps):
        keep[:rows] = tile[0]
        keep[rows:] = jnp.where(end, halo[0], nxt[0])
        out = taps[3:4] * keep[:rows]
        for k in range(3):
            out = out + taps[k : k + 1] * keep[3 - k : 3 - k + rows]
        return out.astype(BF)

    f = tok[0].astype(F32)
    scale = lax.rsqrt(jnp.mean(f * f, -1, keepdims=True) + EPSILON)
    nm = (f * scale * gain[...]).astype(BF)
    dz = dzr[0]
    dx = conv(dpx, nxx, hax, xs, cvx[...])
    db = conv(dpb, nxb, hab, bs, cvb[...])
    low = split_dup(nt(dz, upz[0]) + nt(dx, upx[0]), rank)
    out = nt(dz, wz[...]) + nt(dx, wx[...]) + nt(db, wbc[...]) + nt(ddt[0], wst[...])
    out = out + mm(low, dn[0])
    dg = out * gain[...]
    stat = jnp.sum(dg * f, -1, keepdims=True) / f.shape[1]
    own, other = halves(scale * dg - f * (scale * scale * scale * stat), head[0])
    kept[0] = own + halves(cot[0].astype(F32), head[0])[0]
    send[0] = other
    giz[0] += fold(tn(lrh[0], dz), rank)
    gix[0] += fold(tn(lrh[0], dx), rank)
    gid[0] += fold(tn(low, nm), rank)


def shift(x, axis, by):
    count = lax.axis_size(axis)
    return lax.ppermute(x, axis, [(i, i + by) for i in range(count) if 0 <= i + by < count])


def exchange_kernel(
    giz, gix, god, gid, gou, idx, out, pair, index, got, got2, s1, r1, s2, r2, s3, r3, s4, r4, s5, r5,
    s6, r6,
):
    nz, nb = lax.axis_size("seq"), lax.axis_size("batch")
    z, h, b = lax.axis_index("seq"), lax.axis_index("head"), lax.axis_index("batch")
    rows = giz.shape[0]
    w = giz.shape[1] // nz
    w2 = gid.shape[1] // (2 * nz)

    def plus(i, by, n):
        return lax.rem(i + by, n)

    def cut(p):
        return pl.ds(pl.multiple_of(p * w, w), w)

    def cut2(p, q):
        return pl.ds(pl.multiple_of((q * nz + p) * w2, w2), w2)

    def copy(src, dst, send, recv, **where):
        return pltpu.make_async_remote_copy(
            src_ref=src, dst_ref=dst, send_sem=send, recv_sem=recv, device_id=where,
            device_id_type=pl.DeviceIdType.MESH,
        )

    barrier = pltpu.get_barrier_semaphore()
    pairs = [(d, e) for d in range(nz) for e in range(2) if d or e]
    for d, e in pairs:
        pl.semaphore_signal(
            barrier, inc=1, device_id={"seq": plus(z, d, nz), "head": plus(h, e, 2)},
            device_id_type=pl.DeviceIdType.MESH,
        )
    for f in range(1, nb):
        pl.semaphore_signal(
            barrier, inc=1, device_id={"batch": plus(b, f, nb)},
            device_id_type=pl.DeviceIdType.MESH,
        )
    pl.semaphore_wait(barrier, len(pairs) + nb - 1)

    first = []
    for d in range(1, nz):
        p = plus(z, d, nz)
        for k, ref in enumerate((giz, gix, god)):
            first.append(copy(ref.at[:, cut(p)], got.at[k, d], s1.at[k, d], r1.at[k, d], seq=p))
    for i, (d, e) in enumerate(pairs):
        p, q = plus(z, d, nz), plus(h, e, 2)
        for k, ref in enumerate((gid, gou)):
            first.append(
                copy(ref.at[:, cut2(p, q)], got2.at[k, i], s2.at[k, i], r2.at[k, i], seq=p, head=q)
            )
    for f in range(1, nb):
        first.append(copy(idx, index.at[b], s3.at[f], r3.at[f], batch=plus(b, f, nb)))
    for c in first:
        c.start()
    index[b] = idx[...]
    for c in first:
        c.wait_recv()
    for k, ref in enumerate((giz, gix, god)):
        total = ref[:, cut(z)]
        for d in range(1, nz):
            total = total + got[k, d]
        out[b, z, k * rows : (k + 1) * rows] = total.astype(BF)
    parts = []
    for k, ref in enumerate((gid, gou)):
        total = ref[:, cut2(z, h)]
        for i in range(len(pairs)):
            total = total + got2[k, i]
        parts.append(total.astype(BF))
    out[b, z, 3 * rows :] = jnp.concatenate(parts, 1)
    for c in first:
        c.wait_send()

    sent = []

    def ship(k, src):
        for f in range(1, nb):
            c = copy(src, src, s5.at[k, f], r5.at[k, f], batch=plus(b, f, nb))
            c.start()
            sent.append(c)

    own = out.at[b, z]
    for d in range(1, nz):
        c = copy(own, own, s4.at[d], r4.at[d], seq=plus(z, d, nz))
        c.start()
        sent.append(c)
    ship(0, own)
    for d in range(1, nz):
        there = out.at[b, plus(z, nz - d, nz)]
        copy(there, there, s4.at[d], r4.at[d], seq=plus(z, d, nz)).wait_recv()
        ship(d, there)
    for d in range(nz):
        for f in range(1, nb):
            there = out.at[plus(b, nb - f, nb), plus(z, nz - d, nz)]
            copy(there, there, s5.at[d, f], r5.at[d, f], batch=plus(b, f, nb)).wait_recv()
    for c in sent:
        c.wait_send()
    last = copy(out.at[:, :, pl.ds(3 * rows, rows)], pair, s6, r6, head=plus(h, 1, 2))
    last.start()
    last.wait()


def table_kernel(idx, head, out, pair, up, od, idn, oup, *, seqs):
    nb, nz, _, w = out.shape
    rows = pair.shape[2]
    rank = od.shape[1]
    w2 = w // 2
    h = head[0]
    for ref in (up, od, idn, oup):
        ref[...] = jnp.zeros_like(ref)
    for b in range(nb):
        for s in range(seqs):
            a = idx[b * seqs + s]
            for z in range(nz):

                def part(ref, k):
                    return ref[b, z, k * rows + s * rank : k * rows + (s + 1) * rank].astype(F32)

                cols = slice(z * w, (z + 1) * w)
                up[a, 0, :, cols] += part(out, 0)
                up[a, 1, :, cols] += part(out, 1)
                od[a, :, cols] += part(out, 2)
                mine, other = part(out, 3), part(pair, 0)
                for q, v in ((0, jnp.where(h == 0, mine, other)), (1, jnp.where(h == 0, other, mine))):
                    cols = slice((q * nz + z) * w2, (q * nz + z + 1) * w2)
                    idn[a, :, cols] += v[:, :w2]
                    oup[a, :, cols] += v[:, w2:]


def exchange(giz, gix, god, gid, gou, adapter_index, head, adapters):
    S, R, I = giz.shape
    D = gid.shape[2]
    nz, nb = lax.axis_size("seq"), lax.axis_size("batch")
    rows = S * R
    w, w2 = I // nz, D // (2 * nz)
    if 2 * w2 != w:
        raise ValueError("widths differ")
    sds = jax.ShapeDtypeStruct
    dma = pltpu.SemaphoreType.DMA
    vmem = pl.BlockSpec(memory_space=pltpu.VMEM)
    smem = pl.BlockSpec(memory_space=pltpu.SMEM)
    flat = [v.reshape(rows, v.shape[2]) for v in (giz, gix, god, gid, gou)]
    idx = jnp.zeros((8, LANES), F32).at[0, :S].set(adapter_index.astype(F32))
    others = 2 * nz - 1
    out, pair, index = pl.pallas_call(
        exchange_kernel,
        in_specs=[vmem] * 6,
        out_specs=[vmem] * 3,
        out_shape=[sds((nb, nz, 4 * rows, w), BF), sds((nb, nz, rows, w), BF), sds((nb, 8, LANES), F32)],
        scratch_shapes=[
            pltpu.VMEM((3, nz, rows, w), F32), pltpu.VMEM((2, others, rows, w2), F32),
            dma((3, nz)), dma((3, nz)), dma((2, others)), dma((2, others)), dma((nb,)), dma((nb,)),
            dma((nz,)), dma((nz,)), dma((nz, nb)), dma((nz, nb)), dma, dma,
        ],
        compiler_params=pltpu.CompilerParams(collective_id=0, has_side_effects=True),
        name="exchange",
    )(*flat, idx)
    where = index[:, 0, :S].reshape(nb * S).astype(jnp.int32)
    up, od, idn, oup = pl.pallas_call(
        functools.partial(table_kernel, seqs=S),
        in_specs=[smem, smem, vmem, vmem],
        out_specs=[vmem] * 4,
        out_shape=[sds((adapters, 2, R, I), F32), sds((adapters, R, I), F32),
                   sds((adapters, R, D), F32), sds((adapters, R, D), F32)],
        compiler_params=pltpu.CompilerParams(vmem_limit_bytes=VMEM_LIMIT),
        name="tables",
    )(where, head, out, pair)
    return (jnp.swapaxes(idn, 1, 2), jnp.swapaxes(up, 1, 2), jnp.swapaxes(od, 1, 2), oup)


def local(
    tokens, cotangent, adapter_index, norm_gain, gate_input_weight, bc_weight, step_weight,
    conv_x, conv_bc, dt_bias, a_log, skip_gain, out_gain, output_weight,
    in_down, in_up, out_down, out_up,
):
    S, L, D = tokens.shape
    H = dt_bias.shape[0]
    I = output_weight.shape[0]
    N = bc_weight.shape[2] * lax.axis_size("head")
    NA = in_down.shape[0]
    R = in_down.shape[2]
    hp = I // H
    n_seq = lax.axis_size("seq")
    n_head = lax.axis_size("head")
    full = float(I * n_head)
    TB = min(256, L)
    half = D // n_head

    def swap(v):
        return lax.ppermute(v, "head", [(0, 1), (1, 0)])

    Q = CHUNK
    nc = L // Q
    HR = max(8, -(-H // 8) * 8)
    sds = jax.ShapeDtypeStruct

    UW = min(256, 2 * D)
    wz, wx = pl.pallas_call(
        unweave_kernel,
        grid=(2 * D // UW,),
        in_specs=[pl.BlockSpec((UW, I), lambda t: (t, 0))],
        out_specs=[pl.BlockSpec((UW // 2, I), lambda t: (t, 0))] * 2,
        out_shape=[sds((D, I), BF)] * 2,
        compiler_params=params(1),
        name="unweave",
    )(gate_input_weight.reshape(2 * D, I))
    head = lax.axis_index("head").astype(jnp.int32)[None]
    smem = pl.BlockSpec(memory_space=pltpu.SMEM)
    wbc = lax.all_gather(bc_weight, "head", axis=2, tiled=True).reshape(D, 2 * N)
    cvb = lax.all_gather(conv_bc, "head", axis=2, tiled=True).reshape(conv_bc.shape[0], 2 * N)
    wst = jnp.pad(step_weight, ((0, 0), (0, LANES - H)))
    onehot = (adapter_index[:, None] == jnp.arange(NA)[None, :]).astype(BF)

    def stack(rows):
        return jnp.concatenate(
            [rows, rows, jnp.zeros((S, LANES - 2 * R, rows.shape[2]), BF)], 1
        )

    def pick(spec, table):
        return jnp.einsum(spec, onehot, table, preferred_element_type=F32).astype(BF)

    dn = stack(pick("sa,adr->srd", in_down))
    up = pick("sa,arki->skri", in_up)
    upz = stack(up[:, 0])
    upx = stack(up[:, 1])
    od = stack(pick("sa,air->sri", out_down))
    ou = stack(pick("sa,ard->srd", out_up))
    emap = (jnp.arange(LANES)[:, None] == (jnp.arange(I) // hp)[None, :]).astype(BF)
    spread = jnp.concatenate([emap, emap], 0)

    def lanes(v):
        return jnp.pad(v, (0, LANES - H))[None]

    bias = lanes(dt_bias)
    na = lanes(-jnp.exp(a_log) * LOG2E)
    skip = jnp.repeat(skip_gain, hp)[None]
    gain = norm_gain[None]
    og = out_gain[None]

    def rows(width, tb, order=None):
        f = (lambda s, t: (s, t, 0)) if order is None else (lambda s, t: (s, order(t), 0))
        return pl.BlockSpec((1, tb, width), f)

    def whole(shape):
        return pl.BlockSpec(shape, lambda s, t: (0,) * len(shape))

    def per_seq(shape):
        return pl.BlockSpec((1,) + shape, lambda s, t: (s,) + (0,) * len(shape))

    def chunk4(a, b_, order=None):
        f = (lambda s, t: (s, t, 0, 0)) if order is None else (lambda s, t: (s, order(t), 0, 0))
        return pl.BlockSpec((1, 1, a, b_), f)

    halo = shift(tokens[:, L - HALO :], "seq", 1)
    per = TB // HALO
    grid = (S, L // TB)
    z, xc, slx, bcc, slb, dtr, lrh = pl.pallas_call(
        functools.partial(front_kernel, rank=R),
        grid=grid,
        in_specs=[
            rows(D, TB),
            pl.BlockSpec((1, HALO, D), lambda s, t: (s, jnp.maximum(t * per - 1, 0), 0)),
            per_seq((HALO, D)),
            whole((1, D)), whole((D, I)), whole((D, I)), whole((D, 2 * N)), whole((D, LANES)),
            per_seq((LANES, D)), per_seq((LANES, I)), per_seq((LANES, I)),
            whole(conv_x.shape), whole(cvb.shape),
        ],
        out_specs=[rows(I, TB), rows(I, TB), rows(I, TB), rows(2 * N, TB), rows(2 * N, TB),
                   rows(LANES, TB), rows(LANES, TB)],
        out_shape=[sds((S, L, I), BF), sds((S, L, I), BF), sds((S, L, I), F32),
                   sds((S, L, 2 * N), BF), sds((S, L, 2 * N), F32),
                   sds((S, L, LANES), F32), sds((S, L, LANES), BF)],
        scratch_shapes=[pltpu.VMEM((TB + HALO, I), F32), pltpu.VMEM((TB + HALO, 2 * N), F32)],
        compiler_params=params(2),
        name="front",
    )(tokens, tokens, halo, gain, wz, wx, wbc, wst, dn, upz, upx, conv_x, cvb)

    cgrid = (S, nc)
    tspec = pl.BlockSpec((1, HR, Q), lambda s, t: (s, 0, t))
    cum, vv, rc, cumT, vT, rs, sc, send = pl.pallas_call(
        state_kernel,
        grid=cgrid,
        in_specs=[rows(LANES, Q), rows(I, Q), rows(2 * N, Q), whole((1, LANES)), whole((1, LANES)),
                  whole((2 * LANES, I))],
        out_specs=[rows(LANES, Q), rows(LANES, Q), rows(LANES, Q), tspec, tspec,
                   chunk4(8, LANES), chunk4(N, I), per_seq((N + 16, I))],
        out_shape=[sds((S, L, LANES), F32)] * 3 + [sds((S, HR, L), F32)] * 2
        + [sds((S, nc, 8, LANES), F32), sds((S, nc, N, I), F32), sds((S, N + 16, I), BF)],
        scratch_shapes=[pltpu.VMEM((N, I), F32), pltpu.VMEM((8, LANES), F32)],
        compiler_params=params(2),
        name="states",
    )(dtr, xc, bcc, bias, na, spread)

    def gathered(v):
        return lax.all_gather(v, "seq")

    mine = lax.axis_index("seq")
    all_states = gathered(send)
    decays = (all_states[:, :, N : N + 1] .astype(F32) + all_states[:, :, N + 8 : N + 9].astype(F32))
    sin = jnp.zeros((S, N, I), F32)
    for p in range(n_seq - 1):
        sin = jnp.where(p < mine, sin * decays[p] + all_states[p, :, :N].astype(F32), sin)

    yl = pl.pallas_call(
        functools.partial(intra_kernel, heads=H),
        grid=cgrid,
        in_specs=[rows(I, Q), rows(2 * N, Q), rows(LANES, Q), tspec, chunk4(N, I), whole((1, I)),
                  whole((2 * LANES, I))],
        out_specs=rows(I, Q),
        out_shape=sds((S, L, I), F32),
        compiler_params=params(2),
        cost_estimate=pl.CostEstimate(
            flops=S * L * I * 8 * Q, bytes_accessed=S * L * I * 12, transcendentals=S * L * H * Q
        ),
        name="intra",
    )(xc, bcc, cum, vT, sc, skip, spread)

    dno, blh = pl.pallas_call(
        functools.partial(dnormout_kernel, rank=R),
        grid=grid,
        in_specs=[rows(D, TB), whole((I, D)), per_seq((LANES, I)), per_seq((LANES, D))],
        out_specs=[rows(I, TB), rows(LANES, TB)],
        out_shape=[sds((S, L, I), F32), sds((S, L, LANES), BF)],
        compiler_params=params(2),
        cost_estimate=pl.CostEstimate(
            flops=2 * S * L * I * D, bytes_accessed=S * L * (4 * I + 2 * D), transcendentals=0
        ),
        name="dnormout",
    )(cotangent, output_weight, od, ou)

    sums = pl.pallas_call(
        sums_kernel,
        grid=grid,
        in_specs=[rows(I, TB), rows(2 * N, TB), rows(LANES, TB), per_seq((N, I)), rows(I, TB),
                  rows(I, TB), whole((1, I)), whole((2 * LANES, I))],
        out_specs=rows(LANES, TB),
        out_shape=sds((S, L, LANES), F32),
        compiler_params=params(2),
        name="sums",
    )(yl, bcc, rc, sin, z, dno, og, spread)
    sums = lax.psum(sums[:, :, :2], "head")

    back = lambda t: nc - 1 - t
    no, dzr, dy, dc, dsend = pl.pallas_call(
        functools.partial(gate_back_kernel, full=full),
        grid=cgrid,
        in_specs=[rows(I, Q, back), rows(2 * N, Q, back), rows(LANES, Q, back), rows(LANES, Q, back),
                  per_seq((N, I)), rows(I, Q, back), rows(I, Q, back), rows(2, Q, back),
                  whole((1, I)), whole((2 * LANES, I))],
        out_specs=[rows(I, Q, back), rows(I, Q, back), rows(I, Q, back), chunk4(N, I, back),
                   per_seq((N, I))],
        out_shape=[sds((S, L, I), BF), sds((S, L, I), BF), sds((S, L, I), F32), sds((S, nc, N, I), F32), sds((S, N, I), BF)],
        scratch_shapes=[pltpu.VMEM((N, I), F32)],
        compiler_params=params(2),
        name="gate_back",
    )(yl, bcc, rc, cum, sin, z, dno, sums, og, spread)

    all_returned = gathered(dsend)
    dret = jnp.zeros((S, N, I), F32)
    for p in range(n_seq - 1, 0, -1):
        dret = jnp.where(p > mine, dret * decays[p] + all_returned[p].astype(F32), dret)

    keep, send_mix, god, gou = pl.pallas_call(
        functools.partial(out_kernel, rank=R),
        grid=grid,
        in_specs=[smem, rows(I, TB), rows(D, TB), rows(D, TB), whole((I, D)), per_seq((LANES, I)),
                  per_seq((LANES, D)), rows(LANES, TB)],
        out_specs=[rows(half, TB), rows(half, TB), per_seq((R, I)), per_seq((R, D))],
        out_shape=[sds((S, L, half), F32), sds((S, L, half), BF), sds((S, R, I), F32), sds((S, R, D), F32)],
        compiler_params=params(2),
        cost_estimate=pl.CostEstimate(
            flops=2 * S * L * I * D, bytes_accessed=S * L * (2 * I + 4 * D), transcendentals=0
        ),
        name="out_proj",
    )(head, no, cotangent, tokens, output_weight, od, ou, blh)
    result = (keep + swap(send_mix).astype(F32)).astype(BF)

    total = jnp.broadcast_to(rc[:, L - 1 : L], (S, 8, LANES))
    dpx, dpb, ddt = pl.pallas_call(
        functools.partial(scan_back_kernel, heads=H),
        grid=cgrid,
        in_specs=[rows(I, Q), rows(2 * N, Q), rows(I, Q), tspec, rows(LANES, Q), rows(LANES, Q),
                  rows(LANES, Q), chunk4(8, LANES), chunk4(N, I), per_seq((N, I)), chunk4(N, I),
                  per_seq((N, I)), per_seq((8, LANES)), rows(LANES, Q), whole((1, LANES)),
                  whole((1, LANES)), whole((1, I)), rows(I, Q), rows(2 * N, Q), whole((LANES, I)),
                  whole((2 * LANES, I))],
        out_specs=[rows(I, Q), rows(2 * N, Q), rows(LANES, Q)],
        out_shape=[sds((S, L, I), F32), sds((S, L, 2 * N), F32), sds((S, L, LANES), BF)],
        scratch_shapes=[pltpu.VMEM((LANES, Q), F32)],
        compiler_params=params(2),
        name="scan_back",
    )(xc, bcc, dy, cumT, cum, vv, rc, rs, sc, sin, dc, dret, total, dtr, bias, na, skip, slx, slb,
      emap, spread)

    hax = shift(dpx[:, :HALO], "seq", -1)
    hab = shift(dpb[:, :HALO], "seq", -1)
    last = L // HALO - 1
    after = lambda s, t: (s, jnp.minimum((t + 1) * per, last), 0)
    kept, send_grad, giz, gix, gid = pl.pallas_call(
        functools.partial(back_kernel, rank=R),
        grid=grid,
        in_specs=[
            smem, rows(I, TB), pl.BlockSpec((1, HALO, I), after), per_seq((HALO, I)),
            rows(2 * N, TB), pl.BlockSpec((1, HALO, 2 * N), after), per_seq((HALO, 2 * N)),
            rows(I, TB), rows(LANES, TB), rows(D, TB), rows(D, TB), whole((1, D)), rows(LANES, TB),
            whole((D, I)), whole((D, I)), whole((D, 2 * N)), whole((D, LANES)),
            per_seq((LANES, D)), per_seq((LANES, I)), per_seq((LANES, I)),
            whole(conv_x.shape), whole(cvb.shape),
        ],
        out_specs=[rows(half, TB), rows(half, TB), per_seq((R, I)), per_seq((R, I)),
                   per_seq((R, D))],
        out_shape=[sds((S, L, half), F32), sds((S, L, half), F32), sds((S, R, I), F32),
                   sds((S, R, I), F32), sds((S, R, D), F32)],
        scratch_shapes=[pltpu.VMEM((TB + HALO, I), F32), pltpu.VMEM((TB + HALO, 2 * N), F32)],
        compiler_params=params(2),
        name="in_back",
    )(head, dpx, dpx, hax, dpb, dpb, hab, dzr, ddt, tokens, cotangent, gain, lrh, wz, wx, wbc, wst, dn, upz, upx,
      conv_x, cvb)

    grad_tokens = (kept + swap(send_grad)).astype(BF)

    if n_head == 2 and I % (LANES * n_seq) == 0 and D % (2 * LANES * n_seq) == 0 and R % 16 == 0 and n_head * I == 2 * D:
        sums_of = exchange(giz, gix, god, gid, gou, adapter_index, head, NA)
        return (result, grad_tokens) + sums_of

    heads_part = jnp.stack([giz, gix, god], 1)
    shared_part = jnp.stack([gid, gou], 1)
    heads_part = lax.all_gather(lax.psum(heads_part, "seq"), "batch")
    shared_part = lax.all_gather(lax.psum(shared_part, ("seq", "head")), "batch")
    index = lax.all_gather(adapter_index, "batch")
    chosen = (index[:, :, None] == jnp.arange(NA)).astype(F32)

    def table(part):
        return jnp.einsum("bsa,bskri->akri", chosen, part, precision=lax.Precision.HIGHEST)

    heads_sum = table(heads_part)
    shared_sum = table(shared_part)
    grad_in_up = jnp.swapaxes(heads_sum[:, :2], 1, 2)
    grad_out_down = jnp.swapaxes(heads_sum[:, 2], 1, 2)
    grad_in_down = jnp.swapaxes(shared_sum[:, 0], 1, 2)
    grad_out_up = shared_sum[:, 1]
    return (result, grad_tokens, grad_in_down, grad_in_up, grad_out_down, grad_out_up)


def solution(mesh):
    in_specs = (
        P("batch", "seq", None),
        P("batch", "seq", None),
        P("batch"),
        P(),
        P(None, None, "head"),
        P(None, None, "head"),
        P(None, "head"),
        P(None, "head"),
        P(None, None, "head"),
        P("head"),
        P("head"),
        P("head"),
        P("head"),
        P("head", None),
        P(),
        P(None, None, None, "head"),
        P(None, "head", None),
        P(),
    )
    out_specs = (
        P("batch", "seq", "head"),
        P("batch", "seq", "head"),
        P(),
        P(None, None, None, "head"),
        P(None, "head", None),
        P(),
    )
    return jax.shard_map(local, mesh=mesh, in_specs=in_specs, out_specs=out_specs, check_vma=False)
```

time: 1440 us -> 414 us (0.29)
  matrix products: 490 us -> 4.88 us
  local copies, waits for them, and re-layouts: 297 us -> 20.9 us
  Pallas kernels: 0 us -> 263 us
  other arithmetic: 273 us -> 19.7 us
  waiting for transfers between devices: 302 us -> 68.4 us
  loops' own time: 21.6 us -> 0 us
    dot_general x87 -> x4, matrix products: 490 us -> 4.88 us  [pick(): jnp.einsum(spec, onehot, table, preferred_element_type=F32).astype(BF)]
    pallas_call x0 -> x12, Pallas kernels: none -> 263 us  [the longest x1 48.9 us: local(): pl.pallas_call(functools.partial(scan_back_kernel, heads=H), grid=cgrid,...]
    psum x3 -> x0, waiting for transfers between devices: 225 us -> none  [the longest x1 118 us: local(): lax.psum((local_sums[0], local_sums[1]), ('seq', 'batch'))]
    another operation x45 -> x2, other arithmetic: 105 us -> 0.02 us  [the longest x1 0.02 us: local(): dret * decays[p] + all_returned[p].astype(F32)]
    another operation x68 -> x2, local copies, waits for them, and re-layouts: 59.1 us -> 0.67 us  [the longest x1 0.67 us: local(): skip = jnp.repeat(skip_gain, hp)[None]]
    squeeze x21 -> x1, local copies, waits for them, and re-layouts: 45.7 us -> 0.01 us  [local(): upx = stack(up[:, 1])]
    reshape x7 -> x2, local copies, waits for them, and re-layouts: 53.5 us -> 8.19 us  [the longest x1 7.2 us: local(): gate_input_weight.reshape(2 * D, I)]
    mul x16 -> x1, other arithmetic: 38.3 us -> 0.01 us  [local(): na = lanes(-jnp.exp(a_log) * LOG2E)]
  transfers between devices with their start and end apart: 12 -> 7, of which waited for: 7 -> 4; matrix products, arithmetic and copies ran while one was open for 23% -> 7% of each run, Pallas kernels for 0% -> 24%
where the time goes in v1:
time: 414 us; the launch traced here: 411 us
  Pallas kernels  263 us (64%)
  waiting for transfers between devices  68.4 us (17%)
  local copies, waits for them, and re-layouts  20.9 us (5%)
  other arithmetic  19.7 us (5%)
  between operations  14.4 us (3%)
  blocking collectives  11.4 us (3%)
  starting transfers between devices  8.21 us (2%)
  matrix products  4.88 us (1%)
    all_gather x2, waiting for transfers between devices, gathered(): return lax.all_gather(v, 'seq')  59.9 us
    pallas_call x1, Pallas kernels, local(): pl.pallas_call(functools.partial(scan_back_kernel, heads=H), grid=cgrid,...  48.9 us
    pallas_call x1, Pallas kernels, exchange(): pl.pallas_call(exchange_kernel, in_specs=[vmem] * 6, out_specs=[vmem] * 3...  37.8 us
    pallas_call x1, Pallas kernels, local(): pl.pallas_call(functools.partial(front_kernel, rank=R), grid=grid, in_spe...  31.3 us
    pallas_call x1, Pallas kernels, local(): pl.pallas_call(functools.partial(back_kernel, rank=R), grid=grid, in_spec...  26.7 us
    pallas_call x1, Pallas kernels, local(): pl.pallas_call(functools.partial(gate_back_kernel, full=full), grid=cgrid...  26.4 us
    pallas_call x1, Pallas kernels, local(): pl.pallas_call(functools.partial(intra_kernel, heads=H), grid=cgrid, in_s...  19.3 us
    pallas_call x1, Pallas kernels, local(): pl.pallas_call(state_kernel, grid=cgrid, in_specs=[rows(LANES, Q), rows(I...  18.1 us
  transfers between devices with their start and end apart: 7, of which 4 were waited for; matrix products, arithmetic and copies ran while one was open for 7% of the time, Pallas kernels for 24%

profile of v1, /device:TPU:0, one launch (start us, length us, event | category | flops | bytes accessed | tf_op | source)
XLA Modules:
  0.0 410.9 jit_solution(10963336803776373347)
XLA Ops:
  7.2 0.0 copy-start
  7.2 0.0 all-gather.5.cloned.1.call-start
  7.2 0.9 slice.78
  8.1 4.9 %collective-permute-start = (bf16[2,16,1024]{2,1,0:T(8,128)(2,1)S(1)}, bf16[2,16,1024]{2,1,0:T(8,128)(2,1)S(1)}, u32[]{:S(2)}, u32[]{:S(2)}) collective-permute-start(bf16[2,16,1024]{2,1,0:T(8,128)(2,1)S(1)} %slice.78), channel_id=1, source_target_pairs={{0,8},{8,16},{16,24},{1,9},{9,17},{17,25},{2,10},{10,18},{18,26},{... | collective-permute-start | bytes 196616 | tf_op jit(solution)/shard_map/ppermute | solution.py:404
  13.1 1.1 fusion.8
  14.3 1.3 fusion.13
  15.5 1.3 fusion.15
  16.8 1.3 fusion.11
  18.1 7.2 %reshape.101.w = bf16[2048,1024]{1,0:T(8,128)(2,1)} reshape(bf16[1024,2,1024]{2,1,0:T(2,128)(2,1)} %param.24) | data formatting | bytes 8388608 | tf_op jit(solution)/shard_map/reshape | solution.py:611
  25.3 7.4 %unweave.1 = (bf16[1024,1024]{1,0:T(8,128)(2,1)}, bf16[1024,1024]{1,0:T(8,128)(2,1)}) custom-call(bf16[2048,1024]{1,0:T(8,128)(2,1)} %reshape.101.w), custom_call_target="tpu_custom_call" | custom-call | tf_op jit(solution)/shard_map/unweave/pallas_call | solution.py:603
  32.8 2.3 all_gather.18
  35.1 1.0 copy.60.wbc
  36.1 0.2 copy.47
  36.2 0.1 copy.52
  36.4 1.9 all_gather.19
  38.3 0.1 copy.53
  38.3 0.6 copy.91
  39.0 0.1 fusion.10.emap
  39.0 0.9 pad_maximum_fusion.spread
  40.0 0.8 pad.16.wst
  40.7 0.1 pad.35.clone
  40.8 1.7 maximum_maximum_fusion.4
  42.5 0.6 pad_bitcast_fusion
  43.1 0.6 copy-done.5
  43.8 31.3 %front.1 = (bf16[2,1024,1024]{2,1,0:T(8,128)(2,1)}, bf16[2,1024,1024]{2,1,0:T(8,128)(2,1)}, f32[2,1024,1024]{2,1,0:T(8,128)}, bf16[2,1024,256]{2,1,0:T(8,128)(2,...) custom-call(bf16[2,1024,1024]{2,1,0:T(8,128)(2,1)} %tok.5, ...), custom_call_target="tpu_custom_call" | custom-call | tf_op jit(solution)/shard_map/front/pallas_call | solution.py:662
  75.1 18.1 %states.1 = (f32[2,1024,128]{2,1,0:T(8,128)}, f32[2,1024,128]{2,1,0:T(8,128)}, f32[2,1024,128]{2,1,0:T(8,128)}, f32[2,16,1024]{2,1,0:T(8,128)}, f32[2,16,1024]{2...) custom-call(f32[2,1024,128]{2,1,0:T(8,128)} %get-tuple-element.65.dtr, ...), custom_call_target="tpu_custom_call" | custom-call | tf_op jit(solution)/shard_map/states/pallas_call | solution.py:685
  93.1 0.0 all-gather.5.cloned.1.call-update
  93.2 0.0 all-gather.7.cloned.1.call-start
  93.2 0.1 broadcast_in_dim.34
  93.3 0.7 broadcast_in_dim_reshape.3.skip
  94.0 14.3 %dnormout.1 = (f32[2,1024,1024]{2,1,0:T(8,128)}, bf16[2,1024,128]{2,1,0:T(8,128)(2,1)}) custom-call(bf16[2,1024,1024]{2,1,0:T(8,128)(2,1)} %cot.1, bf16[1024,1024]{1,0:T(8,128)(2,1)} %wo.3, bf16[2,128,1024]{2,1,0:T(8,128)(2,1)} %get-tuple-element.131.od, bf16[2,128,1024]{2,1,0:T(8,128)(2,1)} %get-tuple-element.128.ou), custom_call_target="tpu_custom_call" | custom-call | flops 4294967296 | bytes 12582912 | tf_op jit(solution)/shard_map/dnormout/pallas_call | solution.py:723
  108.2 19.3 %intra.1.yl = f32[2,1024,1024]{2,1,0:T(8,128)} custom-call(bf16[2,1024,1024]{2,1,0:T(8,128)(2,1)} %get-tuple-element.63.xc, bf16[2,1024,256]{2,1,0:T(8,128)(2,1)} %get-tuple-element.64.bcc, f32[2,1024,128]{2,1,0:T(8,128)} %get-tuple-element.66.cum, f32[2,16,1024]{2,1,0:T(8,128)} %get-tuple-element.67.vT, f32[2,8,128,1024]{3,2,1,0:T(8,128)} %get-tuple-element.68.sc, ...), custom_call_target="tpu_custom_call" | custom-call | flops 2147483648 | bytes 25165824 | tf_op jit(solution)/shard_map/intra/pallas_call | solution.py:709
  127.6 16.0 %all-gather.5.cloned.1.call-done = bf16[8,144,1024]{2,1,0:T(8,128)(2,1)} async-done(((bf16[2,144,1024]{2,1,0:T(8,128)(2,1)}), bf16[8,144,1024]{2,1,0:T(8,128)(2,1)}) %all-gather.5.cloned.1.call-update) | async-done | bytes 2359312 | tf_op jit(solution)/shard_map/all_gather | solution.py:700
  143.5 1.0 fusion.20
  144.6 2.7 fusion.sin
  147.3 13.7 %sums.1 = f32[2,1024,128]{2,1,0:T(8,128)} custom-call(f32[2,1024,1024]{2,1,0:T(8,128)} %intra.1.yl, bf16[2,1024,256]{2,1,0:T(8,128)(2,1)} %get-tuple-element.64.bcc, f32[2,1024,128]{2,1,0:T(8,128)} %get-tuple-element.69.rc, f32[2,128,1024]{2,1,0:T(8,128)} %fusion.sin, bf16[2,1024,1024]{2,1,0:T(8,128)(2,1)} %get-tuple-element.71.z, ...), custom_call_target="tpu_custom_call" | custom-call | tf_op jit(solution)/shard_map/sums/pallas_call | solution.py:736
  161.1 7.2 %psum.7.sums = f32[2,1024,2]{2,1,0:T(8,128)} all-reduce(f32[2,1024,2]{2,1,0:T(8,128)} %bitcast.75), channel_id=1, replica_groups=mesh['seq'=4,'head'=2,'batch'=4] {'head'}, use_global_device_ids=true, to_apply=%region_0.1 | all-reduce | flops 4096 | bytes 32768 | tf_op jit(solution)/shard_map/psum | solution.py:746
  168.3 26.4 %gate_back.1 = (bf16[2,1024,1024]{2,1,0:T(8,128)(2,1)}, bf16[2,1024,1024]{2,1,0:T(8,128)(2,1)}, f32[2,1024,1024]{2,1,0:T(8,128)}, f32[2,8,128,1024]{3,2,1,0:T(8,128)}, bf16[2,128,1024]{2,1,0:T(8,128)(2,1)}) custom-call(f32[2,1024,1024]{2,1,0:T(8,128)} %intra.1.yl, bf16[2,1024,256]{2,1,0:T(8,128)(2,1)} %get-tuple-element.64.bcc, ...), custom_call_target="tpu_custom_call" | custom-call | tf_op jit(solution)/shard_map/gate_back/pallas_call | solution.py:749
  194.6 0.0 all-gather.7.cloned.1.call-update
  194.7 0.7 slice.94
  195.4 43.9 %all-gather.7.cloned.1.call-done = bf16[8,128,1024]{2,1,0:T(8,128)(2,1)} async-done(((bf16[2,128,1024]{2,1,0:T(8,128)(2,1)}), bf16[8,128,1024]{2,1,0:T(8,128)(2,1)}) %all-gather.7.cloned.1.call-update) | async-done | bytes 2097168 | tf_op jit(solution)/shard_map/all_gather | solution.py:700
  239.2 2.7 fusion.4.dret
  241.9 0.6 broadcast_in_dim.37.total
  242.5 48.9 %scan_back.1 = (f32[2,1024,1024]{2,1,0:T(8,128)}, f32[2,1024,256]{2,1,0:T(8,128)}, bf16[2,1024,128]{2,1,0:T(8,128)(2,1)}) custom-call(bf16[2,1024,1024]{2,1,0:T(8,128)(2,1)} %get-tuple-element.63.xc, bf16[2,1024,256]{2,1,0:T(8,128)(2,1)} %get-tuple-element.64.bcc, f32[2,1024,1024]{2,1,0:T(8,128)} %get-tuple-element.77.dy, ...), custom_call_target="tpu_custom_call" | custom-call | tf_op jit(solution)/shard_map/scan_back/pallas_call | solution.py:784
  291.4 0.9 slice.95
  292.3 1.3 collective-permute-start.2
  293.6 0.8 slice.96
  294.4 1.3 collective-permute-start.3
  295.7 5.1 %collective-permute-done.3.hab = f32[2,16,256]{2,1,0:T(8,128)S(1)} collective-permute-done((f32[2,16,256]{2,1,0:T(8,128)S(1)}, f32[2,16,256]{2,1,0:T(8,128)S(1)}, u32[]{:S(2)}, u32[]{:S(2)}) %collective-permute-start.3) | collective-permute-done | bytes 32800 | tf_op jit(solution)/shard_map/ppermute | solution.py:404
  300.8 0.6 copy-done.6
  301.4 0.1 copy-done.4
  301.5 26.7 %in_back.1 = (f32[2,1024,512]{2,1,0:T(8,128)}, f32[2,1024,512]{2,1,0:T(8,128)}, f32[2,16,1024]{2,1,0:T(8,128)}, f32[2,16,1024]{2,1,0:T(8,128)}, f32[2,16,1024]{2,1,0:T(8,128)}) custom-call(s32[1]{0:T(128)} %bitcast.head, f32[2,1024,1024]{2,1,0:T(8,128)} %get-tuple-element.85.dpx.nxx, f32[2,1024,1024]{2,1,0:T(8,128)} %get-tuple-element.85.dpx.nxx, ...), custom_call_target="tpu_custom_call" | custom-call | tf_op jit(solution)/shard_map/in_back/pallas_call | solution.py:804
  328.2 0.1 collective-permute-start.4
  328.3 16.2 %out_proj.1 = (f32[2,1024,512]{2,1,0:T(8,128)}, bf16[2,1024,512]{2,1,0:T(8,128)(2,1)}, f32[2,16,1024]{2,1,0:T(8,128)}, f32[2,16,1024]{2,1,0:T(8,128)}) custom-call(s32[1]{0:T(128)} %bitcast.head, bf16[2,1024,1024]{2,1,0:T(8,128)(2,1)} %get-tuple-element.73.no, bf16[2,1024,1024]{2,1,0:T(8,128)(2,1)} %cot.1, bf16[2,1024,1024]{2,1,0:T(8,128)(2,1)} %tok.5, ...), custom_call_target="tpu_custom_call" | custom-call | flops 4294967296 | bytes 12582912 | tf_op jit(solution)/shard_map/out_proj/pallas_call | solution.py:768
  344.4 0.5 collective-permute-start.1
  345.0 0.6 scatter.4.idx
  345.6 3.4 collective-permute-done.1
  349.0 4.4 %add_convert_fusion.1 = bf16[2,1024,512]{2,1,0:T(8,128)(2,1)} fusion(f32[2,1024,512]{2,1,0:T(8,128)} %get-tuple-element.75, bf16[2,1024,512]{2,1,0:T(8,128)(2,1)S(1)} %collective-permute-done.1), kind=kLoop, calls=%fused_computation.1 | loop fusion | flops 3145728 | bytes 8388608 | tf_op jit(solution)/shard_map/convert_element_type | solution.py:781
  353.3 37.8 %exchange.1 = (bf16[4,4,128,256]{3,2,1,0:T(8,128)(2,1)}, bf16[4,4,32,256]{3,2,1,0:T(8,128)(2,1)}, f32[4,8,128]{2,1,0:T(8,128)}) custom-call(f32[32,1024]{1,0:T(8,128)} %bitcast.81, f32[32,1024]{1,0:T(8,128)} %bitcast.82, f32[32,1024]{1,0:T(8,128)} %bitcast.84, f32[32,1024]{1,0:T(8,128)} %bitcast.83, f32[32,1024]{1,0:T(8,128)} %bitcast.85, f32[8,128]{1,0:T(8,128)} %scatter.4.idx), custom_call_target="tpu_custom_call" | custom-call | tf_op jit(solution)/shard_map/exchange/pallas_call | solution.py:550
  391.1 0.7 convert_reduce_fusion
  391.9 0.6 convert_element_type.120.idx
  392.5 3.0 tables.1
  395.5 3.0 copy.58
  398.5 5.6 %add_convert_fusion = bf16[2,1024,512]{2,1,0:T(8,128)(2,1)} fusion(f32[2,1024,512]{2,1,0:T(8,128)} %get-tuple-element.90, f32[2,1024,512]{2,1,0:T(8,128)} %collective-permute-done.4), kind=kLoop, calls=%fused_computation | loop fusion | flops 2097152 | bytes 10485760 | tf_op jit(solution)/shard_map/convert_element_type | solution.py:825
  (38 shorter events, 0.2 us)
Async XLA Ops:
  7.2 5.9 %copy-start = (bf16[8,16,2,1024]{3,2,1,0:T(2,128)(2,1)S(1)}, bf16[8,16,2,1024]{3,2,1,0:T(2,128)(2,1)}, u32[]{:S(2)}) copy-start(bf16[8,16,2,1024]{3,2,1,0:T(2,128)(2,1)} %param.35) | copy-start | bytes 1572868
  7.2 136.4 %all-gather.5.cloned.1.call-start = ((), (), s32[]{:S(2)}) async-start(), calls=%async_computation | async-start | bytes 2949120 | tf_op jit(solution)/shard_map/all_gather | solution.py:700
  8.1 35.0 %collective-permute-start = (bf16[2,16,1024]{2,1,0:T(8,128)(2,1)S(1)}, bf16[2,16,1024]{2,1,0:T(8,128)(2,1)S(1)}, u32[]{:S(2)}, u32[]{:S(2)}) collective-permute-start(bf16[2,16,1024]{2,1,0:T(8,128)(2,1)S(1)} %slice.78), channel_id=1, source_target_pairs={{0,8},{8,16},{16,24},{1,9},{9,17},{17,25},{2,10},{10,18},{18,26},{... | collective-permute-start | bytes 196616 | tf_op jit(solution)/shard_map/ppermute | solution.py:404
  25.3 7.5 %copy-start.3 = (bf16[1024,2,64]{0,2,1:T(8,128)(2,1)S(1)}, bf16[1024,2,64]{0,2,1:T(8,128)(2,1)}, u32[]{:S(2)}) copy-start(bf16[1024,2,64]{0,2,1:T(8,128)(2,1)} %param.25) | copy-start | bytes 786436
  25.3 10.8 %copy-start.7 = (bf16[1024,16]{0,1:T(8,128)(2,1)S(1)}, bf16[1024,16]{0,1:T(8,128)(2,1)}, u32[]{:S(2)}) copy-start(bf16[1024,16]{0,1:T(8,128)(2,1)} %param.26) | copy-start | bytes 98308
  25.3 10.9 %copy-start.9 = (f32[5,2,64]{2,1,0:T(2,128)S(1)}, f32[5,2,64]{2,1,0:T(2,128)}, u32[]{:S(2)}) copy-start(f32[5,2,64]{2,1,0:T(2,128)} %param.28) | copy-start | bytes 7684
  25.3 14.6 %copy-start.12 = (f32[16]{0:T(128)S(1)}, f32[16]{0:T(128)}, u32[]{:S(2)}) copy-start(f32[16]{0:T(128)} %param.30) | copy-start | bytes 196
  32.8 9.8 %copy-start.11 = (f32[16]{0:T(128)S(1)}, f32[16]{0:T(128)}, u32[]{:S(2)}) copy-start(f32[16]{0:T(128)} %param.29) | copy-start | bytes 196
  39.0 36.0 %copy-start.2 = (bf16[128,1024]{1,0:T(8,128)(2,1)}, bf16[128,1024]{1,0:T(8,128)(2,1)S(1)}, u32[]{:S(2)}) copy-start(bf16[128,1024]{1,0:T(8,128)(2,1)S(1)} %fusion.10.emap) | copy-start | bytes 786436
  43.1 0.6 copy-start.5
  75.1 18.2 %copy-start.10 = (f32[16]{0:T(128)S(1)}, f32[16]{0:T(128)}, u32[]{:S(2)}) copy-start(f32[16]{0:T(128)} %param.31) | copy-start | bytes 196
  93.2 146.1 %all-gather.7.cloned.1.call-start = ((), (), s32[]{:S(2)}) async-start(), calls=%async_computation.1 | async-start | bytes 2621440 | tf_op jit(solution)/shard_map/all_gather | solution.py:700
  292.3 8.5 %collective-permute-start.2 = (f32[2,16,1024]{2,1,0:T(8,128)S(1)}, f32[2,16,1024]{2,1,0:T(8,128)S(1)}, u32[]{:S(2)}, u32[]{:S(2)}) collective-permute-start(f32[2,16,1024]{2,1,0:T(8,128)S(1)} %slice.95), channel_id=1, source_target_pairs={{8,0},{16,8},{24,16},{9,1},{17,9},{25,17},{10,2},{18,10},{26,18},{... | collective-permute-start | bytes 393224 | tf_op jit(solution)/shard_map/ppermute | solution.py:404
  294.4 6.4 %collective-permute-start.3 = (f32[2,16,256]{2,1,0:T(8,128)S(1)}, f32[2,16,256]{2,1,0:T(8,128)S(1)}, u32[]{:S(2)}, u32[]{:S(2)}) collective-permute-start(f32[2,16,256]{2,1,0:T(8,128)S(1)} %slice.96), channel_id=1, source_target_pairs={{8,0},{16,8},{24,16},{9,1},{17,9},{25,17},{10,2},{18,10},{26,18},{... | collective-permute-start | bytes 98312 | tf_op jit(solution)/shard_map/ppermute | solution.py:404
  300.8 0.6 copy-start.6
  300.8 0.7 copy-start.4
  328.2 70.3 %collective-permute-start.4 = (f32[2,1024,512]{2,1,0:T(8,128)}, f32[2,1024,512]{2,1,0:T(8,128)}, u32[]{:S(2)}, u32[]{:S(2)}) collective-permute-start(f32[2,1024,512]{2,1,0:T(8,128)} %get-tuple-element.91), channel_id=1, source_target_pairs={{0,4},{4,0},{1,5},{5,1},{2,6},{6,2},{3,7},{7,3},{8,12},{12,8},{9,1... | collective-permute-start | bytes 12582920 | tf_op jit(solution)/shard_map/ppermute | solution.py:595
  328.3 16.7 %copy-start.8 = (s32[2]{0:T(128)S(1)}, s32[2]{0:T(128)}, u32[]{:S(2)}) copy-start(s32[2]{0:T(128)} %param.22) | copy-start | bytes 28
  344.4 4.5 %collective-permute-start.1 = (bf16[2,1024,512]{2,1,0:T(8,128)(2,1)}, bf16[2,1024,512]{2,1,0:T(8,128)(2,1)S(1)}, u32[]{:S(2)}, u32[]{:S(2)}) collective-permute-start(bf16[2,1024,512]{2,1,0:T(8,128)(2,1)} %get-tuple-element.76), channel_id=1, source_target_pairs={{0,4},{4,0},{1,5},{5,1},{2,6},{6,2},{3,7},{7,3},{8,12},{12,8},{9,1... | collective-permute-start | bytes 6291464 | tf_op jit(solution)/shard_map/ppermute | solution.py:595
  398.5 5.6 %copy-start.1 = (bf16[8,16,2,1024]{3,2,1,0:T(2,128)(2,1)S(1)}, bf16[8,16,2,1024]{3,2,1,0:T(2,128)(2,1)}, u32[]{:S(2)}) copy-start(bf16[8,16,2,1024]{3,2,1,0:T(2,128)(2,1)} %param.35) | copy-start | bytes 1572868
Sparse Core Ops, SparseCore 0:
  93.3 50.2 all-gather.4
  194.8 44.4 all-gather.6

commit v2 on v1

--- a/solution.py
+++ b/solution.py
@@ -229,11 +229,12 @@
     gated = y * (gate * s)
     sq = jnp.sum(gated * gated, -1, keepdims=True)
     tot = jnp.sum(dno[0] * og[...] * gated, -1, keepdims=True)
-    sums[0] = jnp.where(lane_of(sums.shape[1:]) == 0, sq, tot)
+    both_sums = jnp.where(lane_of((sq.shape[0], LANES)) == 0, sq, tot)
+    sums[0] = jnp.transpose(both_sums)[:8]
 
 
 def gate_back_kernel(
-    yl, bcc, rc, cum, sin, z, dno, sums, og, spread, no, dzr, dy, dc, send, dst, *, full
+    yl, bcc, rc, cum, sin, z, dno, mine, other, og, spread, no, dzr, dy, dc, send, dst, *, full
 ):
     step = pl.program_id(1)
     q = CHUNK
@@ -246,8 +247,10 @@
     y, gate, s = gated_of(yl, bcc, rc, sin, z, spread)
     act = gate * s
     gated = y * act
-    r = lax.rsqrt(sums[0][:, 0:1] / full + EPSILON)
-    k = r * r * r * (sums[0][:, 1:2] / full)
+    sums = mine[0] + other[0]
+    sums = jnp.transpose(jnp.concatenate([sums, jnp.zeros((LANES - 8, q), F32)], 0))
+    r = lax.rsqrt(sums[:, 0:1] / full + EPSILON)
+    k = r * r * r * (sums[:, 1:2] / full)
     no[0] = (gated * r * og[...]).astype(BF)
     dg = r * (og[...] * dno[0]) - gated * k
     dzr[0] = (dg * y * (s + act * (1.0 - s))).astype(BF)
@@ -656,6 +659,30 @@
         f = (lambda s, t: (s, t, 0, 0)) if order is None else (lambda s, t: (s, order(t), 0, 0))
         return pl.BlockSpec((1, 1, a, b_), f)
 
+    def staged(kernel, name, one, in_specs, args, outs, prev, scratch=()):
+        def at(spec):
+            if spec.index_map is None:
+                return spec
+            return pl.BlockSpec(spec.block_shape, lambda s, t: spec.index_map(one, t))
+
+        shared = [i for i, o in enumerate(outs) if o[2]] if prev else []
+        n = len(args)
+
+        def body(*refs):
+            kernel(*refs[:n], *refs[n + len(shared) :])
+
+        return pl.pallas_call(
+            body,
+            grid=(1, nc),
+            in_specs=[at(v) for v in in_specs] + [pl.BlockSpec(memory_space=pl.ANY)] * len(shared),
+            out_specs=[at(o[0]) for o in outs],
+            out_shape=[o[1] for o in outs],
+            scratch_shapes=list(scratch),
+            input_output_aliases={n + i: k for i, k in enumerate(shared)},
+            compiler_params=params(2),
+            name=name,
+        )(*args, *[prev[k] for k in shared])
+
     halo = shift(tokens[:, L - HALO :], "seq", 1)
     per = TB // HALO
     grid = (S, L // TB)
@@ -682,29 +709,35 @@
 
     cgrid = (S, nc)
     tspec = pl.BlockSpec((1, HR, Q), lambda s, t: (s, 0, t))
-    cum, vv, rc, cumT, vT, rs, sc, send = pl.pallas_call(
-        state_kernel,
-        grid=cgrid,
-        in_specs=[rows(LANES, Q), rows(I, Q), rows(2 * N, Q), whole((1, LANES)), whole((1, LANES)),
-                  whole((2 * LANES, I))],
-        out_specs=[rows(LANES, Q), rows(LANES, Q), rows(LANES, Q), tspec, tspec,
-                   chunk4(8, LANES), chunk4(N, I), per_seq((N + 16, I))],
-        out_shape=[sds((S, L, LANES), F32)] * 3 + [sds((S, HR, L), F32)] * 2
-        + [sds((S, nc, 8, LANES), F32), sds((S, nc, N, I), F32), sds((S, N + 16, I), BF)],
-        scratch_shapes=[pltpu.VMEM((N, I), F32), pltpu.VMEM((8, LANES), F32)],
-        compiler_params=params(2),
-        name="states",
-    )(dtr, xc, bcc, bias, na, spread)
-
-    def gathered(v):
-        return lax.all_gather(v, "seq")
-
+    lane_rows = (rows(LANES, Q), sds((S, L, LANES), F32), True)
+    head_rows = (tspec, sds((S, HR, L), F32), True)
+    state_outs = [
+        lane_rows, lane_rows, lane_rows, head_rows, head_rows,
+        (chunk4(8, LANES), sds((S, nc, 8, LANES), F32), True),
+        (chunk4(N, I), sds((S, nc, N, I), F32), True),
+        (whole((1, N + 16, I)), sds((1, N + 16, I), BF), False),
+    ]
     mine = lax.axis_index("seq")
-    all_states = gathered(send)
-    decays = (all_states[:, :, N : N + 1] .astype(F32) + all_states[:, :, N + 8 : N + 9].astype(F32))
-    sin = jnp.zeros((S, N, I), F32)
-    for p in range(n_seq - 1):
-        sin = jnp.where(p < mine, sin * decays[p] + all_states[p, :, :N].astype(F32), sin)
+    states, sends = None, []
+    for one in range(S):
+        states = staged(
+            state_kernel, "states", one,
+            [rows(LANES, Q), rows(I, Q), rows(2 * N, Q), whole((1, LANES)), whole((1, LANES)),
+             whole((2 * LANES, I))],
+            (dtr, xc, bcc, bias, na, spread), state_outs, states,
+            (pltpu.VMEM((N, I), F32), pltpu.VMEM((8, LANES), F32)),
+        )
+        sends.append(states[-1])
+    cum, vv, rc, cumT, vT, rs, sc = states[:7]
+    sins, decays = [], []
+    for send in sends:
+        all_states = lax.all_gather(send, "seq")
+        dec = all_states[:, :, N : N + 1].astype(F32) + all_states[:, :, N + 8 : N + 9].astype(F32)
+        sin = jnp.zeros((1, N, I), F32)
+        for p in range(n_seq - 1):
+            sin = jnp.where(p < mine, sin * dec[p] + all_states[p, :, :N].astype(F32), sin)
+        sins.append(sin)
+        decays.append(dec)
 
     yl = pl.pallas_call(
         functools.partial(intra_kernel, heads=H),
@@ -733,37 +766,44 @@
         name="dnormout",
     )(cotangent, output_weight, od, ou)
 
-    sums = pl.pallas_call(
-        sums_kernel,
-        grid=grid,
-        in_specs=[rows(I, TB), rows(2 * N, TB), rows(LANES, TB), per_seq((N, I)), rows(I, TB),
-                  rows(I, TB), whole((1, I)), whole((2 * LANES, I))],
-        out_specs=rows(LANES, TB),
-        out_shape=sds((S, L, LANES), F32),
-        compiler_params=params(2),
-        name="sums",
-    )(yl, bcc, rc, sin, z, dno, og, spread)
-    sums = lax.psum(sums[:, :, :2], "head")
+    one_state = whole((1, N, I))
+    one_sums = pl.BlockSpec((1, 8, Q), lambda s, t: (0, 0, t))
+    totals = []
+    for one in range(S):
+        (part,) = staged(
+            sums_kernel, "sums", one,
+            [rows(I, Q), rows(2 * N, Q), rows(LANES, Q), one_state, rows(I, Q), rows(I, Q),
+             whole((1, I)), whole((2 * LANES, I))],
+            (yl, bcc, rc, sins[one], z, dno, og, spread),
+            [(one_sums, sds((1, 8, L), F32), False)], None,
+        )
+        totals.append((part, swap(part)))
 
     back = lambda t: nc - 1 - t
-    no, dzr, dy, dc, dsend = pl.pallas_call(
-        functools.partial(gate_back_kernel, full=full),
-        grid=cgrid,
-        in_specs=[rows(I, Q, back), rows(2 * N, Q, back), rows(LANES, Q, back), rows(LANES, Q, back),
-                  per_seq((N, I)), rows(I, Q, back), rows(I, Q, back), rows(2, Q, back),
-                  whole((1, I)), whole((2 * LANES, I))],
-        out_specs=[rows(I, Q, back), rows(I, Q, back), rows(I, Q, back), chunk4(N, I, back),
-                   per_seq((N, I))],
-        out_shape=[sds((S, L, I), BF), sds((S, L, I), BF), sds((S, L, I), F32), sds((S, nc, N, I), F32), sds((S, N, I), BF)],
-        scratch_shapes=[pltpu.VMEM((N, I), F32)],
-        compiler_params=params(2),
-        name="gate_back",
-    )(yl, bcc, rc, cum, sin, z, dno, sums, og, spread)
-
-    all_returned = gathered(dsend)
-    dret = jnp.zeros((S, N, I), F32)
-    for p in range(n_seq - 1, 0, -1):
-        dret = jnp.where(p > mine, dret * decays[p] + all_returned[p].astype(F32), dret)
+    back_sums = pl.BlockSpec((1, 8, Q), lambda s, t: (0, 0, nc - 1 - t))
+    back_rows = rows(I, Q, back)
+    gates, returns = None, []
+    for one in range(S):
+        gates = staged(
+            functools.partial(gate_back_kernel, full=full), "gate_back", one,
+            [back_rows, rows(2 * N, Q, back), rows(LANES, Q, back), rows(LANES, Q, back), one_state,
+             back_rows, back_rows, back_sums, back_sums, whole((1, I)), whole((2 * LANES, I))],
+            (yl, bcc, rc, cum, sins[one], z, dno) + totals[one] + (og, spread),
+            [(back_rows, sds((S, L, I), BF), True), (back_rows, sds((S, L, I), BF), True),
+             (back_rows, sds((S, L, I), F32), True),
+             (chunk4(N, I, back), sds((S, nc, N, I), F32), True),
+             (one_state, sds((1, N, I), BF), False)],
+            gates, (pltpu.VMEM((N, I), F32),),
+        )
+        returns.append(gates[-1])
+    no, dzr, dy, dc = gates[:4]
+    drets = []
+    for dsend, dec in zip(returns, decays):
+        all_returned = lax.all_gather(dsend, "seq")
+        dret = jnp.zeros((1, N, I), F32)
+        for p in range(n_seq - 1, 0, -1):
+            dret = jnp.where(p > mine, dret * dec[p] + all_returned[p].astype(F32), dret)
+        drets.append(dret)
 
     keep, send_mix, god, gou = pl.pallas_call(
         functools.partial(out_kernel, rank=R),
@@ -778,24 +818,25 @@
         ),
         name="out_proj",
     )(head, no, cotangent, tokens, output_weight, od, ou, blh)
+
+    total = jnp.broadcast_to(rc[:, L - 1 : L], (S, 8, LANES))
+    drets[0], keep, send_mix = lax.optimization_barrier((drets[0], keep, send_mix))
+    scans = None
+    for one in range(S):
+        scans = staged(
+            functools.partial(scan_back_kernel, heads=H), "scan_back", one,
+            [rows(I, Q), rows(2 * N, Q), rows(I, Q), tspec, rows(LANES, Q), rows(LANES, Q),
+             rows(LANES, Q), chunk4(8, LANES), chunk4(N, I), one_state, chunk4(N, I), one_state,
+             per_seq((8, LANES)), rows(LANES, Q), whole((1, LANES)), whole((1, LANES)), whole((1, I)),
+             rows(I, Q), rows(2 * N, Q), whole((LANES, I)), whole((2 * LANES, I))],
+            (xc, bcc, dy, cumT, cum, vv, rc, rs, sc, sins[one], dc, drets[one], total, dtr, bias, na,
+             skip, slx, slb, emap, spread),
+            [(rows(I, Q), sds((S, L, I), F32), True), (rows(2 * N, Q), sds((S, L, 2 * N), F32), True),
+             (rows(LANES, Q), sds((S, L, LANES), BF), True)],
+            scans, (pltpu.VMEM((LANES, Q), F32),),
+        )
+    dpx, dpb, ddt = scans
     result = (keep + swap(send_mix).astype(F32)).astype(BF)
-
-    total = jnp.broadcast_to(rc[:, L - 1 : L], (S, 8, LANES))
-    dpx, dpb, ddt = pl.pallas_call(
-        functools.partial(scan_back_kernel, heads=H),
-        grid=cgrid,
-        in_specs=[rows(I, Q), rows(2 * N, Q), rows(I, Q), tspec, rows(LANES, Q), rows(LANES, Q),
-                  rows(LANES, Q), chunk4(8, LANES), chunk4(N, I), per_seq((N, I)), chunk4(N, I),
-                  per_seq((N, I)), per_seq((8, LANES)), rows(LANES, Q), whole((1, LANES)),
-                  whole((1, LANES)), whole((1, I)), rows(I, Q), rows(2 * N, Q), whole((LANES, I)),
-                  whole((2 * LANES, I))],
-        out_specs=[rows(I, Q), rows(2 * N, Q), rows(LANES, Q)],
-        out_shape=[sds((S, L, I), F32), sds((S, L, 2 * N), F32), sds((S, L, LANES), BF)],
-        scratch_shapes=[pltpu.VMEM((LANES, Q), F32)],
-        compiler_params=params(2),
-        name="scan_back",
-    )(xc, bcc, dy, cumT, cum, vv, rc, rs, sc, sin, dc, dret, total, dtr, bias, na, skip, slx, slb,
-      emap, spread)
 
     hax = shift(dpx[:, :HALO], "seq", -1)
     hab = shift(dpb[:, :HALO], "seq", -1)

time: 414 us -> 364 us (0.88)
  waiting for transfers between devices: 68.4 us -> 7.53 us
  Pallas kernels: 263 us -> 277 us
  blocking collectives: 11.4 us -> 4.2 us
    all_gather x2 -> x4, waiting for transfers between devices: 59.9 us -> 0.06 us  [the longest x2 0.04 us: local(): all_returned = lax.all_gather(dsend, 'seq')]
    pallas_call x4 -> x8, Pallas kernels: 107 us -> 120 us  [staged(): pl.pallas_call(body, grid=(1, nc), in_specs=[at(v) for v in in_specs] + [...]
    psum x1 -> x0, blocking collectives: 7.16 us -> none  [local(): sums = lax.psum(sums[:, :, :2], 'head')]
    select_n x2 -> x4, other arithmetic: 5.42 us -> 8.49 us  [the longest x2 4.29 us: local(): jnp.where(p < mine, sin * dec[p] + all_states[p, :, :N].astype(F32), sin)]
  transfers between devices with their start and end apart: 7 -> 11, of which waited for: 4 -> 3; matrix products, arithmetic and copies ran while one was open for 7% -> 11% of each run, Pallas kernels for 24% -> 51%
where the time goes in v2:
time: 364 us; the launch traced here: 361 us
  Pallas kernels  277 us (76%)
  other arithmetic  22.4 us (6%)
  local copies, waits for them, and re-layouts  22.1 us (6%)
  between operations  14.1 us (4%)
  starting transfers between devices  9.02 us (2%)
  waiting for transfers between devices  7.53 us (2%)
  matrix products  4.88 us (1%)
  blocking collectives  4.2 us (1%)
    pallas_call x8, Pallas kernels, staged(): pl.pallas_call(body, grid=(1, nc), in_specs=[at(v) for v in in_specs] + [...  120 us
    pallas_call x1, Pallas kernels, exchange(): pl.pallas_call(exchange_kernel, in_specs=[vmem] * 6, out_specs=[vmem] * 3...  38.2 us
    pallas_call x1, Pallas kernels, local(): pl.pallas_call(functools.partial(front_kernel, rank=R), grid=grid, in_spe...  31.3 us
    pallas_call x1, Pallas kernels, local(): pl.pallas_call(functools.partial(back_kernel, rank=R), grid=grid, in_spec...  26.7 us
    pallas_call x1, Pallas kernels, local(): pl.pallas_call(functools.partial(intra_kernel, heads=H), grid=cgrid, in_s...  19.4 us
    pallas_call x1, Pallas kernels, local(): pl.pallas_call(functools.partial(out_kernel, rank=R), grid=grid, in_specs...  16.2 us
    pallas_call x1, Pallas kernels, local(): pl.pallas_call(functools.partial(dnormout_kernel, rank=R), grid=grid, in_...  14.1 us
    ppermute x3, starting transfers between devices, shift(): lax.ppermute(x, axis, [(i, i + by) for i in range(count) if 0 <= i + by <...  7.74 us
  transfers between devices with their start and end apart: 11, of which 3 were waited for; matrix products, arithmetic and copies ran while one was open for 11% of the time, Pallas kernels for 51%

profile of v2, /device:TPU:0, one launch (start us, length us, event | category | flops | bytes accessed | tf_op | source)
XLA Modules:
  0.0 360.8 jit_solution(9504713227081277169)
XLA Ops:
  7.2 0.9 slice.113
  8.1 4.9 %collective-permute-start = (bf16[2,16,1024]{2,1,0:T(8,128)(2,1)S(1)}, bf16[2,16,1024]{2,1,0:T(8,128)(2,1)S(1)}, u32[]{:S(2)}, u32[]{:S(2)}) collective-permute-start(bf16[2,16,1024]{2,1,0:T(8,128)(2,1)S(1)} %slice.113), channel_id=1, source_target_pairs={{0,8},{8,16},{16,24},{1,9},{9,17},{17,25},{2,10},{10,18},{18,26},{... | collective-permute-start | bytes 196616 | tf_op jit(solution)/shard_map/ppermute | solution.py:407
  13.1 1.1 fusion.8
  14.3 1.3 fusion.21
  15.5 1.3 fusion.23
  16.8 1.3 fusion.19
  18.1 7.2 %reshape.693.w = bf16[2048,1024]{1,0:T(8,128)(2,1)} reshape(bf16[1024,2,1024]{2,1,0:T(2,128)(2,1)} %param.24) | data formatting | bytes 8388608 | tf_op jit(solution)/shard_map/reshape | solution.py:614
  25.3 7.4 %unweave.1 = (bf16[1024,1024]{1,0:T(8,128)(2,1)}, bf16[1024,1024]{1,0:T(8,128)(2,1)}) custom-call(bf16[2048,1024]{1,0:T(8,128)(2,1)} %reshape.693.w), custom_call_target="tpu_custom_call" | custom-call | tf_op jit(solution)/shard_map/unweave/pallas_call | solution.py:606
  32.8 2.3 all_gather.30
  35.1 1.0 copy.74.wbc
  36.1 0.2 copy.61
  36.3 0.1 copy.66
  36.4 1.9 all_gather.31
  38.4 0.6 copy.97
  39.0 0.9 pad_maximum_fusion.refs_5_.spread.refs_7_.refs_10_.refs_20_
  40.0 0.8 pad.16.wst
  40.7 0.1 pad.35.clone
  40.8 1.7 maximum_maximum_fusion.4
  42.5 0.6 pad_bitcast_fusion
  43.1 0.6 copy-done.6
  43.8 31.3 %front.1 = (bf16[2,1024,1024]{2,1,0:T(8,128)(2,1)}, bf16[2,1024,1024]{2,1,0:T(8,128)(2,1)}, f32[2,1024,1024]{2,1,0:T(8,128)}, bf16[2,1024,256]{2,1,0:T(8,128)(2,...) custom-call(bf16[2,1024,1024]{2,1,0:T(8,128)(2,1)} %tok.5, ...), custom_call_target="tpu_custom_call" | custom-call | tf_op jit(solution)/shard_map/front/pallas_call | solution.py:689
  75.0 9.9 %states.2 = (f32[2,1024,128]{2,1,0:T(8,128)}, f32[2,1024,128]{2,1,0:T(8,128)}, f32[2,1024,128]{2,1,0:T(8,128)}, f32[2,16,1024]{2,1,0:T(8,128)}, f32[2,16,1024]{2...) custom-call(f32[2,1024,128]{2,1,0:T(8,128)} %get-tuple-element.82.refs_0_.refs_1, ...), custom_call_target="tpu_custom_call" | custom-call | tf_op jit(solution)/shard_map/states/pallas_call | solution.py:674
  85.1 9.9 %states.3 = (f32[2,1024,128]{2,1,0:T(8,128)}, f32[2,1024,128]{2,1,0:T(8,128)}, f32[2,1024,128]{2,1,0:T(8,128)}, f32[2,16,1024]{2,1,0:T(8,128)}, f32[2,16,1024]{2...) custom-call(f32[2,1024,128]{2,1,0:T(8,128)} %get-tuple-element.82.re, ...), custom_call_target="tpu_custom_call", output_to_operand_aliasing={{0}: (6, {}), {1}: (7, {}), {2}: (8, {}), {3}: (9, {}), {4}... | custom-call | tf_op jit(solution)/shard_map/states/pallas_call | solution.py:674
  95.2 0.7 broadcast_in_dim_reshape.3.skip.refs_16_
  95.9 14.1 %dnormout.1 = (f32[2,1024,1024]{2,1,0:T(8,128)}, bf16[2,1024,128]{2,1,0:T(8,128)(2,1)}) custom-call(bf16[2,1024,1024]{2,1,0:T(8,128)(2,1)} %cot.1, bf16[1024,1024]{1,0:T(8,128)(2,1)} %wo.3, bf16[2,128,1024]{2,1,0:T(8,128)(2,1)} %get-tuple-element.173.od, bf16[2,128,1024]{2,1,0:T(8,128)(2,1)} %get-tuple-element.170.ou), custom_call_target="tpu_custom_call" | custom-call | flops 4294967296 | bytes 12582912 | tf_op jit(solution)/shard_map/dnormout/pallas_call | solution.py:756
  110.0 19.4 %intra.1.refs_0_ = f32[2,1024,1024]{2,1,0:T(8,128)} custom-call(bf16[2,1024,1024]{2,1,0:T(8,128)(2,1)} %get-tuple-element.83.refs_1_.xc.refs_0_, bf16[2,1024,256]{2,1,0:T(8,128)(2,1)} %get-tuple-element.84.refs_2_.bcc.refs_1_, f32[2,1024,128]{2,1,0:T(8,128)} %get-tuple-element.93.cum.refs_3_.refs_4_, f32[2,16,1024]{2,1,0:T(8,128)} %get-tuple-element.94.vT, ...), custom_call_target="tpu_custom_call" | custom-call | flops 2147483648 | bytes 25165824 | tf_op jit(solution)/shard_map/intra/pallas_call | solution.py:742
  129.4 0.9 fusion.29
  130.3 2.2 fusion.4.refs_3_.refs_4_.refs_9_
  132.4 9.7 %sums.2.refs_7_ = f32[1,8,1024]{2,1,0:T(8,128)} custom-call(f32[2,1024,1024]{2,1,0:T(8,128)} %intra.1.refs_0_, bf16[2,1024,256]{2,1,0:T(8,128)(2,1)} %get-tuple-element.84.refs_2_.bcc.refs_1_, f32[2,1024,128]{2,1,0:T(8,128)} %get-tuple-element.96.refs_2_.refs_6_, f32[1,128,1024]{2,1,0:T(8,128)} %fusion.4.refs_3_.refs_4_.refs_9_, ...), custom_call_target="tpu_custom_call" | custom-call | tf_op jit(solution)/shard_map/sums/pallas_call | solution.py:674
  142.1 0.2 collective-permute-start.1
  142.3 1.2 collective-permute-done.1.refs_8_
  143.6 0.6 copy-done.9
  144.2 14.6 %gate_back.2 = (bf16[2,1024,1024]{2,1,0:T(8,128)(2,1)}, bf16[2,1024,1024]{2,1,0:T(8,128)(2,1)}, f32[2,1024,1024]{2,1,0:T(8,128)}, f32[2,8,128,1024]{3,2,1,0:T(8,128)}, bf16[1,128,1024]{2,1,0:T(8,128)(2,1)}) custom-call(f32[2,1024,1024]{2,1,0:T(8,128)} %intra.1.refs_0_, bf16[2,1024,256]{2,1,0:T(8,128)(2,1)} %get-tuple-element.84.refs_2_.bcc.refs_1_, ...), custom_call_target="tpu_custom_call" | custom-call | tf_op jit(solution)/shard_map/gate_back/pallas_call | solution.py:674
  158.8 0.2 all-gather.15.cloned.1.call-start
  159.1 0.9 fusion.28
  160.0 2.1 fusion.refs_3_.refs_4_.refs_9_
  162.1 9.7 %sums.3.refs_7_ = f32[1,8,1024]{2,1,0:T(8,128)} custom-call(f32[2,1024,1024]{2,1,0:T(8,128)} %intra.1.refs_0_, bf16[2,1024,256]{2,1,0:T(8,128)(2,1)} %get-tuple-element.84.refs_2_.bcc.refs_1_, f32[2,1024,128]{2,1,0:T(8,128)} %get-tuple-element.96.refs_2_.refs_6_, f32[1,128,1024]{2,1,0:T(8,128)} %fusion.refs_3_.refs_4_.refs_9_, ...), custom_call_target="tpu_custom_call" | custom-call | tf_op jit(solution)/shard_map/sums/pallas_call | solution.py:674
  171.8 0.2 collective-permute-start.2
  172.0 1.2 collective-permute-done.2.refs_8_
  173.3 0.6 copy-done.8
  173.9 14.6 %gate_back.3 = (bf16[2,1024,1024]{2,1,0:T(8,128)(2,1)}, bf16[2,1024,1024]{2,1,0:T(8,128)(2,1)}, f32[2,1024,1024]{2,1,0:T(8,128)}, f32[2,8,128,1024]{3,2,1,0:T(8,128)}, bf16[1,128,1024]{2,1,0:T(8,128)(2,1)}) custom-call(f32[2,1024,1024]{2,1,0:T(8,128)} %intra.1.refs_0_, ...), custom_call_target="tpu_custom_call", output_to_operand_aliasing={{0}: (11, {}), {1}: (12, {}), {2}: (13, {}), {3}: (14, {})} | custom-call | tf_op jit(solution)/shard_map/gate_back/pallas_call | solution.py:674
  188.6 0.7 slice.140
  189.3 16.2 %out_proj.1 = (f32[2,1024,512]{2,1,0:T(8,128)}, bf16[2,1024,512]{2,1,0:T(8,128)(2,1)}, f32[2,16,1024]{2,1,0:T(8,128)}, f32[2,16,1024]{2,1,0:T(8,128)}) custom-call(s32[1]{0:T(128)} %bitcast.21.head, bf16[2,1024,1024]{2,1,0:T(8,128)(2,1)} %get-tuple-element.105.no, bf16[2,1024,1024]{2,1,0:T(8,128)(2,1)} %cot.1, bf16[2,1024,1024]{2,1,0:T(8,128)(2,1)} %tok.5, ...), custom_call_target="tpu_custom_call" | custom-call | flops 4294967296 | bytes 12582912 | tf_op jit(solution)/shard_map/out_proj/pallas_call | solution.py:808
  205.5 2.1 fusion.14.refs_11_
  207.6 0.6 broadcast_in_dim.37.refs_12_
  208.2 25.9 %scan_back.2 = (f32[2,1024,1024]{2,1,0:T(8,128)}, f32[2,1024,256]{2,1,0:T(8,128)}, bf16[2,1024,128]{2,1,0:T(8,128)(2,1)}) custom-call(bf16[2,1024,1024]{2,1,0:T(8,128)(2,1)} %get-tuple-element.83.refs_1_.xc.refs_0_, bf16[2,1024,256]{2,1,0:T(8,128)(2,1)} %get-tuple-element.84.refs_2_.bcc.refs_1_, f32[2,1024,1024]{2,1,0:T(8,128)} %get-tuple-element.111.refs_2_, ...), custom_call_target="tpu_custom_call" | custom-call | tf_op jit(solution)/shard_map/scan_back/pallas_call | solution.py:674
  234.1 2.1 fusion.10.refs_11_
  236.2 25.9 %scan_back.3 = (f32[2,1024,1024]{2,1,0:T(8,128)}, f32[2,1024,256]{2,1,0:T(8,128)}, bf16[2,1024,128]{2,1,0:T(8,128)(2,1)}) custom-call(bf16[2,1024,1024]{2,1,0:T(8,128)(2,1)} %get-tuple-element.83.refs_1_.xc.refs_0_, bf16[2,1024,256]{2,1,0:T(8,128)(2,1)} %get-tuple-element.84.refs_2_.bcc.refs_1_, ...), custom_call_target="tpu_custom_call", output_to_operand_aliasing={{0}: (21, {}), {1}: (22, {}), {2}: (23, {})} | custom-call | tf_op jit(solution)/shard_map/scan_back/pallas_call | solution.py:674
  262.1 0.9 slice.141
  263.0 1.3 collective-permute-start.4
  264.3 0.8 slice.142
  265.0 1.5 collective-permute-start.5
  266.6 4.9 %collective-permute-done.5.hab = f32[2,16,256]{2,1,0:T(8,128)S(1)} collective-permute-done((f32[2,16,256]{2,1,0:T(8,128)S(1)}, f32[2,16,256]{2,1,0:T(8,128)S(1)}, u32[]{:S(2)}, u32[]{:S(2)}) %collective-permute-start.5) | collective-permute-done | bytes 32800 | tf_op jit(solution)/shard_map/ppermute | solution.py:407
  271.5 0.6 copy-done.7
  272.1 26.7 %in_back.1 = (f32[2,1024,512]{2,1,0:T(8,128)}, f32[2,1024,512]{2,1,0:T(8,128)}, f32[2,16,1024]{2,1,0:T(8,128)}, f32[2,16,1024]{2,1,0:T(8,128)}, f32[2,16,1024]{2,1,0:T(8,128)}) custom-call(s32[1]{0:T(128)} %bitcast.21.head, f32[2,1024,1024]{2,1,0:T(8,128)} %get-tuple-element.123.dpx.nxx, f32[2,1024,1024]{2,1,0:T(8,128)} %get-tuple-element.123.dpx.nxx, ...), custom_call_target="tpu_custom_call" | custom-call | tf_op jit(solution)/shard_map/in_back/pallas_call | solution.py:845
  298.9 0.5 collective-permute-start.3
  299.4 0.6 scatter.4.idx
  300.0 38.2 %exchange.1 = (bf16[4,4,128,256]{3,2,1,0:T(8,128)(2,1)}, bf16[4,4,32,256]{3,2,1,0:T(8,128)(2,1)}, f32[4,8,128]{2,1,0:T(8,128)}) custom-call(f32[32,1024]{1,0:T(8,128)} %bitcast.95, f32[32,1024]{1,0:T(8,128)} %bitcast.96, f32[32,1024]{1,0:T(8,128)} %bitcast.93, f32[32,1024]{1,0:T(8,128)} %bitcast.97, f32[32,1024]{1,0:T(8,128)} %bitcast.94, f32[8,128]{1,0:T(8,128)} %scatter.4.idx), custom_call_target="tpu_custom_call" | custom-call | tf_op jit(solution)/shard_map/exchange/pallas_call | solution.py:553
  338.2 0.7 convert_reduce_fusion
  339.0 0.6 convert_element_type.274.idx
  339.6 3.0 tables.1
  342.6 3.0 copy.72
  345.6 4.4 %add_convert_fusion.1 = bf16[2,1024,512]{2,1,0:T(8,128)(2,1)} fusion(f32[2,1024,512]{2,1,0:T(8,128)} %get-tuple-element.109, bf16[2,1024,512]{2,1,0:T(8,128)(2,1)S(1)} %collective-permute-done.3), kind=kLoop, calls=%fused_computation.1 | loop fusion | flops 3145728 | bytes 8388608 | tf_op jit(solution)/shard_map/convert_element_type | solution.py:839
  350.0 4.3 %add_convert_fusion = bf16[2,1024,512]{2,1,0:T(8,128)(2,1)} fusion(f32[2,1024,512]{2,1,0:T(8,128)S(1)} %copy-done.3, f32[2,1024,512]{2,1,0:T(8,128)} %collective-permute-done.6), kind=kLoop, calls=%fused_computation | loop fusion | flops 2097152 | bytes 10485760 | tf_op jit(solution)/shard_map/convert_element_type | solution.py:866
  (57 shorter events, 0.8 us)
Async XLA Ops:
  7.2 5.9 %copy-start = (bf16[8,16,2,1024]{3,2,1,0:T(2,128)(2,1)S(1)}, bf16[8,16,2,1024]{3,2,1,0:T(2,128)(2,1)}, u32[]{:S(2)}) copy-start(bf16[8,16,2,1024]{3,2,1,0:T(2,128)(2,1)} %param.35) | copy-start | bytes 1572868
  7.2 122.2 %all-gather.9.cloned.1.call-start = ((), (), s32[]{:S(2)}) async-start(), calls=%async_computation | async-start | bytes 1474560 | tf_op jit(solution)/shard_map/all_gather | solution.py:734
  8.1 35.0 %collective-permute-start = (bf16[2,16,1024]{2,1,0:T(8,128)(2,1)S(1)}, bf16[2,16,1024]{2,1,0:T(8,128)(2,1)S(1)}, u32[]{:S(2)}, u32[]{:S(2)}) collective-permute-start(bf16[2,16,1024]{2,1,0:T(8,128)(2,1)S(1)} %slice.113), channel_id=1, source_target_pairs={{0,8},{8,16},{16,24},{1,9},{9,17},{17,25},{2,10},{10,18},{18,26},{... | collective-permute-start | bytes 196616 | tf_op jit(solution)/shard_map/ppermute | solution.py:407
  25.3 7.5 %copy-start.4 = (bf16[1024,2,64]{0,2,1:T(8,128)(2,1)S(1)}, bf16[1024,2,64]{0,2,1:T(8,128)(2,1)}, u32[]{:S(2)}) copy-start(bf16[1024,2,64]{0,2,1:T(8,128)(2,1)} %param.25) | copy-start | bytes 786436
  25.3 10.8 %copy-start.10 = (bf16[1024,16]{0,1:T(8,128)(2,1)S(1)}, bf16[1024,16]{0,1:T(8,128)(2,1)}, u32[]{:S(2)}) copy-start(bf16[1024,16]{0,1:T(8,128)(2,1)} %param.26) | copy-start | bytes 98308
  25.3 10.9 %copy-start.12 = (f32[5,2,64]{2,1,0:T(2,128)S(1)}, f32[5,2,64]{2,1,0:T(2,128)}, u32[]{:S(2)}) copy-start(f32[5,2,64]{2,1,0:T(2,128)} %param.28) | copy-start | bytes 7684
  25.3 14.6 %copy-start.15 = (f32[16]{0:T(128)S(1)}, f32[16]{0:T(128)}, u32[]{:S(2)}) copy-start(f32[16]{0:T(128)} %param.30) | copy-start | bytes 196
  32.8 9.8 %copy-start.14 = (f32[16]{0:T(128)S(1)}, f32[16]{0:T(128)}, u32[]{:S(2)}) copy-start(f32[16]{0:T(128)} %param.29) | copy-start | bytes 196
  39.0 36.0 %copy-start.2 = (bf16[128,1024]{1,0:T(8,128)(2,1)}, bf16[128,1024]{1,0:T(8,128)(2,1)S(1)}, u32[]{:S(2)}) copy-start(bf16[128,1024]{1,0:T(8,128)(2,1)S(1)} %fusion.18.refs_19_) | copy-start | bytes 786436
  43.1 0.6 copy-start.6
  85.0 74.1 %all-gather.13.cloned.1.call-start = ((), (), s32[]{:S(2)}) async-start(), calls=%async_computation.2 | async-start | bytes 1474560 | tf_op jit(solution)/shard_map/all_gather | solution.py:734
  85.1 10.0 %copy-start.13 = (f32[16]{0:T(128)S(1)}, f32[16]{0:T(128)}, u32[]{:S(2)}) copy-start(f32[16]{0:T(128)} %param.31) | copy-start | bytes 196
  95.1 110.4 %all-gather.11.cloned.1.call-start = ((), (), s32[]{:S(2)}) async-start(), calls=%async_computation.1 | async-start | bytes 1310720 | tf_op jit(solution)/shard_map/all_gather | solution.py:802
  142.1 1.4 collective-permute-start.1
  143.6 0.6 copy-start.9
  158.8 75.2 %all-gather.15.cloned.1.call-start = ((), (), s32[]{:S(2)}) async-start(), calls=%async_computation.3 | async-start | bytes 1310720 | tf_op jit(solution)/shard_map/all_gather | solution.py:802
  171.8 1.4 collective-permute-start.2
  173.3 0.6 copy-start.8
  263.0 8.5 %collective-permute-start.4 = (f32[2,16,1024]{2,1,0:T(8,128)S(1)}, f32[2,16,1024]{2,1,0:T(8,128)S(1)}, u32[]{:S(2)}, u32[]{:S(2)}) collective-permute-start(f32[2,16,1024]{2,1,0:T(8,128)S(1)} %slice.141), channel_id=1, source_target_pairs={{8,0},{16,8},{24,16},{9,1},{17,9},{25,17},{10,2},{18,10},{26,18},{... | collective-permute-start | bytes 393224 | tf_op jit(solution)/shard_map/ppermute | solution.py:407
  265.0 6.4 %collective-permute-start.5 = (f32[2,16,256]{2,1,0:T(8,128)S(1)}, f32[2,16,256]{2,1,0:T(8,128)S(1)}, u32[]{:S(2)}, u32[]{:S(2)}) collective-permute-start(f32[2,16,256]{2,1,0:T(8,128)S(1)} %slice.142), channel_id=1, source_target_pairs={{8,0},{16,8},{24,16},{9,1},{17,9},{25,17},{10,2},{18,10},{26,18},{... | collective-permute-start | bytes 98312 | tf_op jit(solution)/shard_map/ppermute | solution.py:407
  271.5 0.6 copy-start.7
  271.5 0.7 copy-start.5
  272.1 27.3 %copy-start.11 = (s32[2]{0:T(128)S(1)}, s32[2]{0:T(128)}, u32[]{:S(2)}) copy-start(s32[2]{0:T(128)} %param.22) | copy-start | bytes 28
  298.8 51.1 %collective-permute-start.6 = (f32[2,1024,512]{2,1,0:T(8,128)}, f32[2,1024,512]{2,1,0:T(8,128)}, u32[]{:S(2)}, u32[]{:S(2)}) collective-permute-start(f32[2,1024,512]{2,1,0:T(8,128)} %get-tuple-element.129), channel_id=1, source_target_pairs={{0,4},{4,0},{1,5},{5,1},{2,6},{6,2},{3,7},{7,3},{8,12},{12,8},{9,1... | collective-permute-start | bytes 12582920 | tf_op jit(solution)/shard_map/ppermute | solution.py:598
  298.9 46.7 %collective-permute-start.3 = (bf16[2,1024,512]{2,1,0:T(8,128)(2,1)}, bf16[2,1024,512]{2,1,0:T(8,128)(2,1)S(1)}, u32[]{:S(2)}, u32[]{:S(2)}) collective-permute-start(bf16[2,1024,512]{2,1,0:T(8,128)(2,1)} %get-tuple-element.110), channel_id=1, source_target_pairs={{0,4},{4,0},{1,5},{5,1},{2,6},{6,2},{3,7},{7,3},{8,12},{12,8},{9,1... | collective-permute-start | bytes 6291464 | tf_op jit(solution)/shard_map/ppermute | solution.py:598
  345.6 4.4 %copy-start.3 = (f32[2,1024,512]{2,1,0:T(8,128)S(1)}, f32[2,1024,512]{2,1,0:T(8,128)}, u32[]{:S(2)}) copy-start(f32[2,1024,512]{2,1,0:T(8,128)} %get-tuple-element.128) | copy-start | bytes 12582916
  350.0 4.3 %copy-start.1 = (bf16[8,16,2,1024]{3,2,1,0:T(2,128)(2,1)S(1)}, bf16[8,16,2,1024]{3,2,1,0:T(2,128)(2,1)}, u32[]{:S(2)}) copy-start(bf16[8,16,2,1024]{3,2,1,0:T(2,128)(2,1)} %param.35) | copy-start | bytes 1572868
Sparse Core Ops, SparseCore 0:
  85.1 30.4 all-gather.8
  117.2 29.4 all-gather.12
  159.0 28.2 all-gather.10
  188.7 28.2 all-gather.14

commit v3 on v2

--- a/solution.py
+++ b/solution.py
@@ -106,11 +106,11 @@
 
 
 def unweave_kernel(w, even, odd):
-    n = w.shape[0]
+    n = 2 * w.shape[0]
     r = row_of((n, n))
     c = lane_of((n, n))
     m = (c == jnp.where(r < n // 2, 2 * r, 2 * r - n + 1)).astype(BF)
-    out = mm(m, w[...]).astype(BF)
+    out = mm(m, w[...].reshape(n, w.shape[2])).astype(BF)
     even[...] = out[: n // 2]
     odd[...] = out[n // 2 :]
 
@@ -224,7 +224,19 @@
     return y, gate, s
 
 
-def sums_kernel(yl, bcc, rc, sin, z, dno, og, spread, sums):
+def sums_kernel(place, every, yl, bcc, rc, z, dno, og, spread, sums, sin, decays):
+    n = sin.shape[1]
+
+    @pl.when(pl.program_id(1) == 0)
+    def _():
+        state = jnp.zeros(sin.shape[1:], F32)
+        for p in range(every.shape[0]):
+            dec = every[p, 0, n : n + 1].astype(F32) + every[p, 0, n + 8 : n + 9].astype(F32)
+            decays[p : p + 1] = dec
+            if p < every.shape[0] - 1:
+                state = jnp.where(p < place[0], state * dec + every[p, 0, :n].astype(F32), state)
+        sin[0] = state
+
     y, gate, s = gated_of(yl, bcc, rc, sin, z, spread)
     gated = y * (gate * s)
     sq = jnp.sum(gated * gated, -1, keepdims=True)
@@ -282,9 +294,18 @@
 
 
 def scan_back_kernel(
-    xc, bcc, dy, cumT, cum, vv, rc, rs, sc, sin, dc, dret, total, dtr, bias, na, skip, slx, slb,
-    emap, spread, dpx, dpb, ddt, rowq, *, heads,
+    place, every, decays, xc, bcc, dy, cumT, cum, vv, rc, rs, sc, sin, dc, total, dtr, bias, na, skip,
+    slx, slb, emap, spread, dpx, dpb, ddt, rowq, dret, *, heads,
 ):
+    @pl.when(pl.program_id(1) == 0)
+    def _():
+        state = jnp.zeros(dret.shape, F32)
+        for p in range(every.shape[0] - 1, 0, -1):
+            state = jnp.where(
+                p > place[0], state * decays[p : p + 1] + every[p, 0].astype(F32), state
+            )
+        dret[...] = state
+
     q = CHUNK
     n = bcc.shape[2] // 2
     b = bcc[0][:, :n]
@@ -305,7 +326,7 @@
     )
     decs = expand(jnp.exp2(head8), spread[...])
     s_in = sc[0, 0] + decs[0:1] * sin[0]
-    d_out = dc[0, 0] + decs[1:2] * dret[0]
+    d_out = dc[0, 0] + decs[1:2] * dret[...]
     s_two = parts(s_in)
     d_two = parts(d_out)
     x = xc[0].astype(F32)
@@ -408,7 +429,7 @@
 
 
 def exchange_kernel(
-    giz, gix, god, gid, gou, idx, out, pair, index, got, got2, s1, r1, s2, r2, s3, r3, s4, r4, s5, r5,
+    giz, gix, god, gid, gou, idx, out, pair, index, low, got, got2, s1, r1, s2, r2, s3, r3, s4, r4, s5, r5,
     s6, r6,
 ):
     nz, nb = lax.axis_size("seq"), lax.axis_size("batch")
@@ -432,6 +453,8 @@
             device_id_type=pl.DeviceIdType.MESH,
         )
 
+    for k, ref in enumerate((giz, gix, god, gid, gou)):
+        low[k] = ref[...].astype(BF)
     barrier = pltpu.get_barrier_semaphore()
     pairs = [(d, e) for d in range(nz) for e in range(2) if d or e]
     for d, e in pairs:
@@ -449,13 +472,13 @@
     first = []
     for d in range(1, nz):
         p = plus(z, d, nz)
-        for k, ref in enumerate((giz, gix, god)):
-            first.append(copy(ref.at[:, cut(p)], got.at[k, d], s1.at[k, d], r1.at[k, d], seq=p))
+        for k in range(3):
+            first.append(copy(low.at[k, :, cut(p)], got.at[k, d], s1.at[k, d], r1.at[k, d], seq=p))
     for i, (d, e) in enumerate(pairs):
         p, q = plus(z, d, nz), plus(h, e, 2)
-        for k, ref in enumerate((gid, gou)):
+        for k in range(2):
             first.append(
-                copy(ref.at[:, cut2(p, q)], got2.at[k, i], s2.at[k, i], r2.at[k, i], seq=p, head=q)
+                copy(low.at[3 + k, :, cut2(p, q)], got2.at[k, i], s2.at[k, i], r2.at[k, i], seq=p, head=q)
             )
     for f in range(1, nb):
         first.append(copy(idx, index.at[b], s3.at[f], r3.at[f], batch=plus(b, f, nb)))
@@ -467,13 +490,13 @@
     for k, ref in enumerate((giz, gix, god)):
         total = ref[:, cut(z)]
         for d in range(1, nz):
-            total = total + got[k, d]
+            total = total + got[k, d].astype(F32)
         out[b, z, k * rows : (k + 1) * rows] = total.astype(BF)
     parts = []
     for k, ref in enumerate((gid, gou)):
         total = ref[:, cut2(z, h)]
         for i in range(len(pairs)):
-            total = total + got2[k, i]
+            total = total + got2[k, i].astype(F32)
         parts.append(total.astype(BF))
     out[b, z, 3 * rows :] = jnp.concatenate(parts, 1)
     for c in first:
@@ -556,7 +579,8 @@
         out_specs=[vmem] * 3,
         out_shape=[sds((nb, nz, 4 * rows, w), BF), sds((nb, nz, rows, w), BF), sds((nb, 8, LANES), F32)],
         scratch_shapes=[
-            pltpu.VMEM((3, nz, rows, w), F32), pltpu.VMEM((2, others, rows, w2), F32),
+            pltpu.VMEM((5, rows, I), BF), pltpu.VMEM((3, nz, rows, w), BF),
+            pltpu.VMEM((2, others, rows, w2), BF),
             dma((3, nz)), dma((3, nz)), dma((2, others)), dma((2, others)), dma((nb,)), dma((nb,)),
             dma((nz,)), dma((nz,)), dma((nz, nb)), dma((nz, nb)), dma, dma,
         ],
@@ -606,12 +630,12 @@
     wz, wx = pl.pallas_call(
         unweave_kernel,
         grid=(2 * D // UW,),
-        in_specs=[pl.BlockSpec((UW, I), lambda t: (t, 0))],
+        in_specs=[pl.BlockSpec((UW // 2, 2, I), lambda t: (t, 0, 0))],
         out_specs=[pl.BlockSpec((UW // 2, I), lambda t: (t, 0))] * 2,
         out_shape=[sds((D, I), BF)] * 2,
         compiler_params=params(1),
         name="unweave",
-    )(gate_input_weight.reshape(2 * D, I))
+    )(gate_input_weight)
     head = lax.axis_index("head").astype(jnp.int32)[None]
     smem = pl.BlockSpec(memory_space=pltpu.SMEM)
     wbc = lax.all_gather(bc_weight, "head", axis=2, tiled=True).reshape(D, 2 * N)
@@ -729,15 +753,8 @@
         )
         sends.append(states[-1])
     cum, vv, rc, cumT, vT, rs, sc = states[:7]
-    sins, decays = [], []
-    for send in sends:
-        all_states = lax.all_gather(send, "seq")
-        dec = all_states[:, :, N : N + 1].astype(F32) + all_states[:, :, N + 8 : N + 9].astype(F32)
-        sin = jnp.zeros((1, N, I), F32)
-        for p in range(n_seq - 1):
-            sin = jnp.where(p < mine, sin * dec[p] + all_states[p, :, :N].astype(F32), sin)
-        sins.append(sin)
-        decays.append(dec)
+    place = mine.astype(jnp.int32)[None]
+    every = [lax.all_gather(send, "seq") for send in sends]
 
     yl = pl.pallas_call(
         functools.partial(intra_kernel, heads=H),
@@ -768,16 +785,19 @@
 
     one_state = whole((1, N, I))
     one_sums = pl.BlockSpec((1, 8, Q), lambda s, t: (0, 0, t))
-    totals = []
+    totals, sins, decays = [], [], []
     for one in range(S):
-        (part,) = staged(
+        part, sin, dec = staged(
             sums_kernel, "sums", one,
-            [rows(I, Q), rows(2 * N, Q), rows(LANES, Q), one_state, rows(I, Q), rows(I, Q),
-             whole((1, I)), whole((2 * LANES, I))],
-            (yl, bcc, rc, sins[one], z, dno, og, spread),
-            [(one_sums, sds((1, 8, L), F32), False)], None,
+            [smem, whole((n_seq, 1, N + 16, I)), rows(I, Q), rows(2 * N, Q), rows(LANES, Q), rows(I, Q),
+             rows(I, Q), whole((1, I)), whole((2 * LANES, I))],
+            (place, every[one], yl, bcc, rc, z, dno, og, spread),
+            [(one_sums, sds((1, 8, L), F32), False), (one_state, sds((1, N, I), F32), False),
+             (whole((n_seq, I)), sds((n_seq, I), F32), False)], None,
         )
         totals.append((part, swap(part)))
+        sins.append(sin)
+        decays.append(dec)
 
     back = lambda t: nc - 1 - t
     back_sums = pl.BlockSpec((1, 8, Q), lambda s, t: (0, 0, nc - 1 - t))
@@ -797,14 +817,28 @@
         )
         returns.append(gates[-1])
     no, dzr, dy, dc = gates[:4]
-    drets = []
-    for dsend, dec in zip(returns, decays):
-        all_returned = lax.all_gather(dsend, "seq")
-        dret = jnp.zeros((1, N, I), F32)
-        for p in range(n_seq - 1, 0, -1):
-            dret = jnp.where(p > mine, dret * dec[p] + all_returned[p].astype(F32), dret)
-        drets.append(dret)
-
+    returned = [lax.all_gather(dsend, "seq") for dsend in returns]
+
+    total = jnp.broadcast_to(rc[:, L - 1 : L], (S, 8, LANES))
+    scans = None
+    for one in range(S):
+        scans = staged(
+            functools.partial(scan_back_kernel, heads=H), "scan_back", one,
+            [smem, whole((n_seq, 1, N, I)), whole((n_seq, I)), rows(I, Q), rows(2 * N, Q), rows(I, Q),
+             tspec, rows(LANES, Q), rows(LANES, Q), rows(LANES, Q), chunk4(8, LANES), chunk4(N, I),
+             one_state, chunk4(N, I),
+             per_seq((8, LANES)), rows(LANES, Q), whole((1, LANES)), whole((1, LANES)), whole((1, I)),
+             rows(I, Q), rows(2 * N, Q), whole((LANES, I)), whole((2 * LANES, I))],
+            (place, returned[one], decays[one], xc, bcc, dy, cumT, cum, vv, rc, rs, sc, sins[one], dc, total, dtr, bias, na,
+             skip, slx, slb, emap, spread),
+            [(rows(I, Q), sds((S, L, I), F32), True), (rows(2 * N, Q), sds((S, L, 2 * N), F32), True),
+             (rows(LANES, Q), sds((S, L, LANES), BF), True)],
+            scans, (pltpu.VMEM((LANES, Q), F32), pltpu.VMEM((N, I), F32)),
+        )
+    dpx, dpb, ddt = scans
+    hax = shift(dpx[:, :HALO], "seq", -1)
+    hab = shift(dpb[:, :HALO], "seq", -1)
+    no, ddt = lax.optimization_barrier((no, ddt))
     keep, send_mix, god, gou = pl.pallas_call(
         functools.partial(out_kernel, rank=R),
         grid=grid,
@@ -818,28 +852,8 @@
         ),
         name="out_proj",
     )(head, no, cotangent, tokens, output_weight, od, ou, blh)
-
-    total = jnp.broadcast_to(rc[:, L - 1 : L], (S, 8, LANES))
-    drets[0], keep, send_mix = lax.optimization_barrier((drets[0], keep, send_mix))
-    scans = None
-    for one in range(S):
-        scans = staged(
-            functools.partial(scan_back_kernel, heads=H), "scan_back", one,
-            [rows(I, Q), rows(2 * N, Q), rows(I, Q), tspec, rows(LANES, Q), rows(LANES, Q),
-             rows(LANES, Q), chunk4(8, LANES), chunk4(N, I), one_state, chunk4(N, I), one_state,
-             per_seq((8, LANES)), rows(LANES, Q), whole((1, LANES)), whole((1, LANES)), whole((1, I)),
-             rows(I, Q), rows(2 * N, Q), whole((LANES, I)), whole((2 * LANES, I))],
-            (xc, bcc, dy, cumT, cum, vv, rc, rs, sc, sins[one], dc, drets[one], total, dtr, bias, na,
-             skip, slx, slb, emap, spread),
-            [(rows(I, Q), sds((S, L, I), F32), True), (rows(2 * N, Q), sds((S, L, 2 * N), F32), True),
-             (rows(LANES, Q), sds((S, L, LANES), BF), True)],
-            scans, (pltpu.VMEM((LANES, Q), F32),),
-        )
-    dpx, dpb, ddt = scans
     result = (keep + swap(send_mix).astype(F32)).astype(BF)
 
-    hax = shift(dpx[:, :HALO], "seq", -1)
-    hab = shift(dpb[:, :HALO], "seq", -1)
     last = L // HALO - 1
     after = lambda s, t: (s, jnp.minimum((t + 1) * per, last), 0)
     kept, send_grad, giz, gix, gid = pl.pallas_call(

time: 364 us -> 344 us (0.945)
  other arithmetic: 22.4 us -> 12.2 us
  local copies, waits for them, and re-layouts: 22.1 us -> 14.9 us
  Pallas kernels: 277 us -> 272 us
    select_n x4 -> x0, other arithmetic: 8.49 us -> none  [the longest x2 4.29 us: local(): jnp.where(p < mine, sin * dec[p] + all_states[p, :, :N].astype(F32), sin)]
    reshape x1 -> x0, local copies, waits for them, and re-layouts: 7.22 us -> none  [local(): gate_input_weight.reshape(2 * D, I)]
    pallas_call x1, Pallas kernels: 38.2 us -> 31.1 us  [exchange(): pl.pallas_call(exchange_kernel, in_specs=[vmem] * 6, out_specs=[vmem] * 3...]
  transfers between devices with their start and end apart: 11 -> 11, of which waited for: 3 -> 5; matrix products, arithmetic and copies ran while one was open for 11% -> 7% of each run, Pallas kernels for 51% -> 52%
where the time goes in v3:
time: 344 us; the launch traced here: 341 us
  Pallas kernels  272 us (79%)
  local copies, waits for them, and re-layouts  14.9 us (4%)
  between operations  14.1 us (4%)
  other arithmetic  12.2 us (4%)
  waiting for transfers between devices  9.71 us (3%)
  starting transfers between devices  9.31 us (3%)
  matrix products  4.89 us (1%)
  blocking collectives  4.2 us (1%)
    pallas_call x8, Pallas kernels, staged(): pl.pallas_call(body, grid=(1, nc), in_specs=[at(v) for v in in_specs] + [...  122 us
    pallas_call x1, Pallas kernels, local(): pl.pallas_call(functools.partial(front_kernel, rank=R), grid=grid, in_spe...  31.3 us
    pallas_call x1, Pallas kernels, exchange(): pl.pallas_call(exchange_kernel, in_specs=[vmem] * 6, out_specs=[vmem] * 3...  31.1 us
    pallas_call x1, Pallas kernels, local(): pl.pallas_call(functools.partial(back_kernel, rank=R), grid=grid, in_spec...  26.8 us
    pallas_call x1, Pallas kernels, local(): pl.pallas_call(functools.partial(intra_kernel, heads=H), grid=cgrid, in_s...  19.4 us
    pallas_call x1, Pallas kernels, local(): pl.pallas_call(functools.partial(out_kernel, rank=R), grid=grid, in_specs...  16.1 us
    pallas_call x1, Pallas kernels, local(): pl.pallas_call(functools.partial(dnormout_kernel, rank=R), grid=grid, in_...  14.1 us
    ppermute x3, starting transfers between devices, shift(): lax.ppermute(x, axis, [(i, i + by) for i in range(count) if 0 <= i + by <...  7.87 us
  transfers between devices with their start and end apart: 11, of which 5 were waited for; matrix products, arithmetic and copies ran while one was open for 7% of the time, Pallas kernels for 52%

profile of v3, /device:TPU:0, one launch (start us, length us, event | category | flops | bytes accessed | tf_op | source)
XLA Modules:
  0.0 340.8 jit_solution(11747305596271962593)
XLA Ops:
  7.2 0.9 slice.37
  8.2 5.1 %collective-permute-start = (bf16[2,16,1024]{2,1,0:T(8,128)(2,1)S(1)}, bf16[2,16,1024]{2,1,0:T(8,128)(2,1)S(1)}, u32[]{:S(2)}, u32[]{:S(2)}) collective-permute-start(bf16[2,16,1024]{2,1,0:T(8,128)(2,1)S(1)} %slice.37), channel_id=1, source_target_pairs={{0,8},{8,16},{16,24},{1,9},{9,17},{17,25},{2,10},{10,18},{18,26},{... | collective-permute-start | bytes 196616 | tf_op jit(solution)/shard_map/ppermute | solution.py:428
  13.3 1.1 fusion
  14.4 1.3 fusion.5
  15.7 1.3 fusion.7
  17.0 1.3 fusion.3
  18.3 7.4 %unweave.1 = (bf16[1024,1024]{1,0:T(8,128)(2,1)}, bf16[1024,1024]{1,0:T(8,128)(2,1)}) custom-call(bf16[1024,2,1024]{2,1,0:T(2,128)(2,1)} %w.1), custom_call_target="tpu_custom_call" | custom-call | tf_op jit(solution)/shard_map/unweave/pallas_call | solution.py:630
  25.7 2.3 all_gather.30
  28.0 1.0 copy.74.wbc
  29.0 0.2 copy.61
  29.2 0.1 copy.66
  29.3 1.9 all_gather.31
  31.2 0.1 copy.67
  31.3 0.6 copy.97
  31.9 0.1 fusion.2.refs_21_
  32.0 0.9 pad_maximum_fusion.refs_5_.spread.refs_8_.refs_10_.refs_22_
  32.9 0.8 pad.16.wst
  33.7 0.1 pad.35.clone
  33.8 1.7 maximum_maximum_fusion.4
  35.5 0.6 pad_bitcast_fusion
  36.1 0.6 copy-done.6
  36.7 31.3 %front.1 = (bf16[2,1024,1024]{2,1,0:T(8,128)(2,1)}, bf16[2,1024,1024]{2,1,0:T(8,128)(2,1)}, f32[2,1024,1024]{2,1,0:T(8,128)}, bf16[2,1024,256]{2,1,0:T(8,128)(2,...) custom-call(bf16[2,1024,1024]{2,1,0:T(8,128)(2,1)} %tok.5, ...), custom_call_target="tpu_custom_call" | custom-call | tf_op jit(solution)/shard_map/front/pallas_call | solution.py:713
  68.0 9.9 %states.2 = (f32[2,1024,128]{2,1,0:T(8,128)}, f32[2,1024,128]{2,1,0:T(8,128)}, f32[2,1024,128]{2,1,0:T(8,128)}, f32[2,16,1024]{2,1,0:T(8,128)}, f32[2,16,1024]{2...) custom-call(f32[2,1024,128]{2,1,0:T(8,128)} %get-tuple-element.89.refs_0_.refs_1, ...), custom_call_target="tpu_custom_call" | custom-call | tf_op jit(solution)/shard_map/states/pallas_call | solution.py:698
  78.0 9.9 %states.3 = (f32[2,1024,128]{2,1,0:T(8,128)}, f32[2,1024,128]{2,1,0:T(8,128)}, f32[2,1024,128]{2,1,0:T(8,128)}, f32[2,16,1024]{2,1,0:T(8,128)}, f32[2,16,1024]{2...) custom-call(f32[2,1024,128]{2,1,0:T(8,128)} %get-tuple-element.89.re, ...), custom_call_target="tpu_custom_call", output_to_operand_aliasing={{0}: (6, {}), {1}: (7, {}), {2}: (8, {}), {3}: (9, {}), {4}... | custom-call | tf_op jit(solution)/shard_map/states/pallas_call | solution.py:698
  88.0 0.1 broadcast_in_dim.37
  88.1 0.7 broadcast_in_dim_reshape.3.skip.refs_18_
  88.8 14.1 %dnormout.1 = (f32[2,1024,1024]{2,1,0:T(8,128)}, bf16[2,1024,128]{2,1,0:T(8,128)(2,1)}) custom-call(bf16[2,1024,1024]{2,1,0:T(8,128)(2,1)} %cot.1, bf16[1024,1024]{1,0:T(8,128)(2,1)} %wo.3, bf16[2,128,1024]{2,1,0:T(8,128)(2,1)} %get-tuple-element.175.od, bf16[2,128,1024]{2,1,0:T(8,128)(2,1)} %get-tuple-element.172.ou), custom_call_target="tpu_custom_call" | custom-call | flops 4294967296 | bytes 12582912 | tf_op jit(solution)/shard_map/dnormout/pallas_call | solution.py:773
  102.9 19.4 %intra.1.refs_2_.refs_0_ = f32[2,1024,1024]{2,1,0:T(8,128)} custom-call(bf16[2,1024,1024]{2,1,0:T(8,128)(2,1)} %get-tuple-element.87.refs_1_.xc.refs_3_, bf16[2,1024,256]{2,1,0:T(8,128)(2,1)} %get-tuple-element.88.refs_2_.bcc.refs_3_.refs_1_.refs_4_, f32[2,1024,128]{2,1,0:T(8,128)} %get-tuple-element.97.cum.refs_3_.refs_7_, ...), custom_call_target="tpu_custom_call" | custom-call | flops 2147483648 | bytes 25165824 | tf_op jit(solution)/shard_map/intra/pallas_call | solution.py:759
  122.3 10.3 %sums.3 = (f32[1,8,1024]{2,1,0:T(8,128)}, f32[1,128,1024]{2,1,0:T(8,128)}, f32[4,1024]{1,0:T(4,128)}) custom-call(s32[1]{0:T(128)} %bitcast.12.refs_0_, bf16[4,1,144,1024]{3,2,1,0:T(8,128)(2,1)} %bitcast.53, f32[2,1024,1024]{2,1,0:T(8,128)} %intra.1.refs_2_.refs_0_, bf16[2,1024,256]{2,1,0:T(8,128)(2,1)} %get-tuple-element.88.refs_2_.bcc.refs_3_.refs_1_.refs_4_, ...), custom_call_target="tpu_custom_call" | custom-call | tf_op jit(solution)/shard_map/sums/pallas_call | solution.py:698
  132.6 0.3 collective-permute-start.2
  132.8 1.2 collective-permute-done.2.refs_8_
  134.1 0.6 copy-done.9
  134.6 14.6 %gate_back.2 = (bf16[2,1024,1024]{2,1,0:T(8,128)(2,1)}, bf16[2,1024,1024]{2,1,0:T(8,128)(2,1)}, f32[2,1024,1024]{2,1,0:T(8,128)}, f32[2,8,128,1024]{3,2,1,0:T(8,128)}, bf16[1,128,1024]{2,1,0:T(8,128)(2,1)}) custom-call(f32[2,1024,1024]{2,1,0:T(8,128)} %intra.1.refs_2_.refs_0_, bf16[2,1024,256]{2,1,0:T(8,128)(2,1)} %get-tuple-element.88.refs_2_.bcc.refs_3_.refs_1_.refs_4_, ...), custom_call_target="tpu_custom_call" | custom-call | tf_op jit(solution)/shard_map/gate_back/pallas_call | solution.py:698
  149.3 0.2 all-gather.13.cloned.1.call-start
  149.6 10.4 %sums.2 = (f32[1,8,1024]{2,1,0:T(8,128)}, f32[1,128,1024]{2,1,0:T(8,128)}, f32[4,1024]{1,0:T(4,128)}) custom-call(s32[1]{0:T(128)} %bitcast.12.refs_0_, bf16[4,1,144,1024]{3,2,1,0:T(8,128)(2,1)} %bitcast.52, f32[2,1024,1024]{2,1,0:T(8,128)} %intra.1.refs_2_.refs_0_, bf16[2,1024,256]{2,1,0:T(8,128)(2,1)} %get-tuple-element.88.refs_2_.bcc.refs_3_.refs_1_.refs_4_, ...), custom_call_target="tpu_custom_call" | custom-call | tf_op jit(solution)/shard_map/sums/pallas_call | solution.py:698
  160.0 0.2 collective-permute-start.1
  160.2 1.3 collective-permute-done.1.refs_8_
  161.5 0.6 copy-done.8
  162.1 14.6 %gate_back.3 = (bf16[2,1024,1024]{2,1,0:T(8,128)(2,1)}, bf16[2,1024,1024]{2,1,0:T(8,128)(2,1)}, f32[2,1024,1024]{2,1,0:T(8,128)}, f32[2,8,128,1024]{3,2,1,0:T(8,128)}, bf16[1,128,1024]{2,1,0:T(8,128)(2,1)}) custom-call(f32[2,1024,1024]{2,1,0:T(8,128)} %intra.1.refs_2_.refs_0_, ...), custom_call_target="tpu_custom_call", output_to_operand_aliasing={{0}: (11, {}), {1}: (12, {}), {2}: (13, {}), {3}: (14, {})} | custom-call | tf_op jit(solution)/shard_map/gate_back/pallas_call | solution.py:698
  176.7 0.7 slice.40
  177.4 0.3 all-gather.15.cloned.1.call-done
  177.8 0.6 broadcast_in_dim.41.refs_14_
  178.4 26.3 %scan_back.2 = (f32[2,1024,1024]{2,1,0:T(8,128)}, f32[2,1024,256]{2,1,0:T(8,128)}, bf16[2,1024,128]{2,1,0:T(8,128)(2,1)}) custom-call(s32[1]{0:T(128)} %bitcast.12.refs_0_, bf16[4,1,128,1024]{3,2,1,0:T(8,128)(2,1)} %bitcast.55, f32[4,1024]{1,0:T(4,128)} %get-tuple-element.124.refs_2_, bf16[2,1024,1024]{2,1,0:T(8,128)(2,1)} %get-tuple-element.87.refs_1_.xc.refs_3_, ...), custom_call_target="tpu_custom_call" | custom-call | tf_op jit(solution)/shard_map/scan_back/pallas_call | solution.py:698
  204.7 1.9 all-gather.13.cloned.1.call-done
  206.6 26.3 %scan_back.3 = (f32[2,1024,1024]{2,1,0:T(8,128)}, f32[2,1024,256]{2,1,0:T(8,128)}, bf16[2,1024,128]{2,1,0:T(8,128)(2,1)}) custom-call(s32[1]{0:T(128)} %bitcast.12.refs_0_, bf16[4,1,128,1024]{3,2,1,0:T(8,128)(2,1)} %bitcast.54, f32[4,1024]{1,0:T(4,128)} %get-tuple-element.115.refs_2_, ...), custom_call_target="tpu_custom_call", output_to_operand_aliasing={{0}: (23, {}), {1}: (24, {}), {2}: (25, {})} | custom-call | tf_op jit(solution)/shard_map/scan_back/pallas_call | solution.py:698
  232.9 0.9 slice.41
  233.8 1.3 collective-permute-start.4
  235.1 0.8 slice.42
  235.9 1.5 collective-permute-start.5
  237.4 4.9 %collective-permute-done.5.hab = f32[2,16,256]{2,1,0:T(8,128)S(1)} collective-permute-done((f32[2,16,256]{2,1,0:T(8,128)S(1)}, f32[2,16,256]{2,1,0:T(8,128)S(1)}, u32[]{:S(2)}, u32[]{:S(2)}) %collective-permute-start.5) | collective-permute-done | bytes 32800 | tf_op jit(solution)/shard_map/ppermute | solution.py:428
  242.3 0.6 copy-done.7
  242.9 0.1 copy-done.5
  242.9 26.8 %in_back.1 = (f32[2,1024,512]{2,1,0:T(8,128)}, f32[2,1024,512]{2,1,0:T(8,128)}, f32[2,16,1024]{2,1,0:T(8,128)}, f32[2,16,1024]{2,1,0:T(8,128)}, f32[2,16,1024]{2,1,0:T(8,128)}) custom-call(s32[1]{0:T(128)} %bitcast.head, f32[2,1024,1024]{2,1,0:T(8,128)} %get-tuple-element.133.dpx.nxx, f32[2,1024,1024]{2,1,0:T(8,128)} %get-tuple-element.133.dpx.nxx, ...), custom_call_target="tpu_custom_call" | custom-call | tf_op jit(solution)/shard_map/in_back/pallas_call | solution.py:859
  269.8 0.1 collective-permute-start.6
  269.9 16.1 %out_proj.1 = (f32[2,1024,512]{2,1,0:T(8,128)}, bf16[2,1024,512]{2,1,0:T(8,128)(2,1)}, f32[2,16,1024]{2,1,0:T(8,128)}, f32[2,16,1024]{2,1,0:T(8,128)}) custom-call(s32[1]{0:T(128)} %bitcast.head, bf16[2,1024,1024]{2,1,0:T(8,128)(2,1)} %get-tuple-element.129.no, bf16[2,1024,1024]{2,1,0:T(8,128)(2,1)} %cot.1, bf16[2,1024,1024]{2,1,0:T(8,128)(2,1)} %tok.5, ...), custom_call_target="tpu_custom_call" | custom-call | flops 4294967296 | bytes 12582912 | tf_op jit(solution)/shard_map/out_proj/pallas_call | solution.py:842
  286.0 0.5 collective-permute-start.3
  286.6 0.6 scatter.4.idx
  287.2 31.1 %exchange.1 = (bf16[4,4,128,256]{3,2,1,0:T(8,128)(2,1)}, bf16[4,4,32,256]{3,2,1,0:T(8,128)(2,1)}, f32[4,8,128]{2,1,0:T(8,128)}) custom-call(f32[32,1024]{1,0:T(8,128)} %bitcast.58, f32[32,1024]{1,0:T(8,128)} %bitcast.59, f32[32,1024]{1,0:T(8,128)} %bitcast.61, f32[32,1024]{1,0:T(8,128)} %bitcast.60, f32[32,1024]{1,0:T(8,128)} %bitcast.62, f32[8,128]{1,0:T(8,128)} %scatter.4.idx), custom_call_target="tpu_custom_call" | custom-call | tf_op jit(solution)/shard_map/exchange/pallas_call | solution.py:576
  318.2 0.7 convert_reduce_fusion
  319.0 0.6 convert_element_type.66.idx
  319.6 3.0 tables.1
  322.6 3.0 copy.72
  325.6 4.4 %add_convert_fusion.1 = bf16[2,1024,512]{2,1,0:T(8,128)(2,1)} fusion(f32[2,1024,512]{2,1,0:T(8,128)} %get-tuple-element.131, bf16[2,1024,512]{2,1,0:T(8,128)(2,1)S(1)} %collective-permute-done.3), kind=kLoop, calls=%fused_computation.1 | loop fusion | flops 3145728 | bytes 8388608 | tf_op jit(solution)/shard_map/convert_element_type | solution.py:855
  330.0 4.3 %add_convert_fusion = bf16[2,1024,512]{2,1,0:T(8,128)(2,1)} fusion(f32[2,1024,512]{2,1,0:T(8,128)S(1)} %copy-done.3, f32[2,1024,512]{2,1,0:T(8,128)} %collective-permute-done.6), kind=kLoop, calls=%fused_computation | loop fusion | flops 2097152 | bytes 10485760 | tf_op jit(solution)/shard_map/convert_element_type | solution.py:880
  (48 shorter events, 0.4 us)
Async XLA Ops:
  7.2 6.1 %copy-start = (bf16[8,16,2,1024]{3,2,1,0:T(2,128)(2,1)S(1)}, bf16[8,16,2,1024]{3,2,1,0:T(2,128)(2,1)}, u32[]{:S(2)}) copy-start(bf16[8,16,2,1024]{3,2,1,0:T(2,128)(2,1)} %param.35) | copy-start | bytes 1572868
  7.2 18.5 %copy-start.4 = (bf16[1024,2,64]{0,2,1:T(8,128)(2,1)S(1)}, bf16[1024,2,64]{0,2,1:T(8,128)(2,1)}, u32[]{:S(2)}) copy-start(bf16[1024,2,64]{0,2,1:T(8,128)(2,1)} %param.25) | copy-start | bytes 786436
  7.2 115.1 %all-gather.11.cloned.1.call-start = ((), (), s32[]{:S(2)}) async-start(), calls=%async_computation.1 | async-start | bytes 1474560 | tf_op jit(solution)/shard_map/all_gather | solution.py:757
  8.2 20.8 %copy-start.10 = (bf16[1024,16]{0,1:T(8,128)(2,1)S(1)}, bf16[1024,16]{0,1:T(8,128)(2,1)}, u32[]{:S(2)}) copy-start(bf16[1024,16]{0,1:T(8,128)(2,1)} %param.26) | copy-start | bytes 98308
  8.2 28.0 %collective-permute-start = (bf16[2,16,1024]{2,1,0:T(8,128)(2,1)S(1)}, bf16[2,16,1024]{2,1,0:T(8,128)(2,1)S(1)}, u32[]{:S(2)}, u32[]{:S(2)}) collective-permute-start(bf16[2,16,1024]{2,1,0:T(8,128)(2,1)S(1)} %slice.37), channel_id=1, source_target_pairs={{0,8},{8,16},{16,24},{1,9},{9,17},{17,25},{2,10},{10,18},{18,26},{... | collective-permute-start | bytes 196616 | tf_op jit(solution)/shard_map/ppermute | solution.py:428
  13.3 15.9 %copy-start.12 = (f32[5,2,64]{2,1,0:T(2,128)S(1)}, f32[5,2,64]{2,1,0:T(2,128)}, u32[]{:S(2)}) copy-start(f32[5,2,64]{2,1,0:T(2,128)} %param.28) | copy-start | bytes 7684
  17.0 15.9 %copy-start.15 = (f32[16]{0:T(128)S(1)}, f32[16]{0:T(128)}, u32[]{:S(2)}) copy-start(f32[16]{0:T(128)} %param.30) | copy-start | bytes 196
  25.7 9.8 %copy-start.14 = (f32[16]{0:T(128)S(1)}, f32[16]{0:T(128)}, u32[]{:S(2)}) copy-start(f32[16]{0:T(128)} %param.29) | copy-start | bytes 196
  32.0 36.0 %copy-start.2 = (bf16[128,1024]{1,0:T(8,128)(2,1)}, bf16[128,1024]{1,0:T(8,128)(2,1)S(1)}, u32[]{:S(2)}) copy-start(bf16[128,1024]{1,0:T(8,128)(2,1)S(1)} %fusion.2.refs_21_) | copy-start | bytes 786436
  36.1 0.6 copy-start.6
  77.9 71.6 %all-gather.9.cloned.1.call-start = ((), (), s32[]{:S(2)}) async-start(), calls=%async_computation | async-start | bytes 1474560 | tf_op jit(solution)/shard_map/all_gather | solution.py:757
  78.0 10.0 %copy-start.13 = (f32[16]{0:T(128)S(1)}, f32[16]{0:T(128)}, u32[]{:S(2)}) copy-start(f32[16]{0:T(128)} %param.31) | copy-start | bytes 196
  87.9 89.8 %all-gather.15.cloned.1.call-start = ((), (), s32[]{:S(2)}) async-start(), calls=%async_computation.3 | async-start | bytes 1310720 | tf_op jit(solution)/shard_map/all_gather | solution.py:820
  132.6 1.5 collective-permute-start.2
  134.0 0.6 copy-start.9
  149.3 57.3 %all-gather.13.cloned.1.call-start = ((), (), s32[]{:S(2)}) async-start(), calls=%async_computation.2 | async-start | bytes 1310720 | tf_op jit(solution)/shard_map/all_gather | solution.py:820
  160.0 1.5 collective-permute-start.1
  161.5 0.6 copy-start.8
  233.8 8.5 %collective-permute-start.4 = (f32[2,16,1024]{2,1,0:T(8,128)S(1)}, f32[2,16,1024]{2,1,0:T(8,128)S(1)}, u32[]{:S(2)}, u32[]{:S(2)}) collective-permute-start(f32[2,16,1024]{2,1,0:T(8,128)S(1)} %slice.41), channel_id=1, source_target_pairs={{8,0},{16,8},{24,16},{9,1},{17,9},{25,17},{10,2},{18,10},{26,18},{... | collective-permute-start | bytes 393224 | tf_op jit(solution)/shard_map/ppermute | solution.py:428
  235.9 6.4 %collective-permute-start.5 = (f32[2,16,256]{2,1,0:T(8,128)S(1)}, f32[2,16,256]{2,1,0:T(8,128)S(1)}, u32[]{:S(2)}, u32[]{:S(2)}) collective-permute-start(f32[2,16,256]{2,1,0:T(8,128)S(1)} %slice.42), channel_id=1, source_target_pairs={{8,0},{16,8},{24,16},{9,1},{17,9},{25,17},{10,2},{18,10},{26,18},{... | collective-permute-start | bytes 98312 | tf_op jit(solution)/shard_map/ppermute | solution.py:428
  242.3 0.6 copy-start.7
  242.3 0.7 copy-start.5
  269.8 60.2 %collective-permute-start.6 = (f32[2,1024,512]{2,1,0:T(8,128)}, f32[2,1024,512]{2,1,0:T(8,128)}, u32[]{:S(2)}, u32[]{:S(2)}) collective-permute-start(f32[2,1024,512]{2,1,0:T(8,128)} %get-tuple-element.139), channel_id=1, source_target_pairs={{0,4},{4,0},{1,5},{5,1},{2,6},{6,2},{3,7},{7,3},{8,12},{12,8},{9,1... | collective-permute-start | bytes 12582920 | tf_op jit(solution)/shard_map/ppermute | solution.py:622
  269.9 16.7 %copy-start.11 = (s32[2]{0:T(128)S(1)}, s32[2]{0:T(128)}, u32[]{:S(2)}) copy-start(s32[2]{0:T(128)} %param.22) | copy-start | bytes 28
  286.0 39.6 %collective-permute-start.3 = (bf16[2,1024,512]{2,1,0:T(8,128)(2,1)}, bf16[2,1024,512]{2,1,0:T(8,128)(2,1)S(1)}, u32[]{:S(2)}, u32[]{:S(2)}) collective-permute-start(bf16[2,1024,512]{2,1,0:T(8,128)(2,1)} %get-tuple-element.132), channel_id=1, source_target_pairs={{0,4},{4,0},{1,5},{5,1},{2,6},{6,2},{3,7},{7,3},{8,12},{12,8},{9,1... | collective-permute-start | bytes 6291464 | tf_op jit(solution)/shard_map/ppermute | solution.py:622
  325.6 4.4 %copy-start.3 = (f32[2,1024,512]{2,1,0:T(8,128)S(1)}, f32[2,1024,512]{2,1,0:T(8,128)}, u32[]{:S(2)}) copy-start(f32[2,1024,512]{2,1,0:T(8,128)} %get-tuple-element.138) | copy-start | bytes 12582916
  330.0 4.3 %copy-start.1 = (bf16[8,16,2,1024]{3,2,1,0:T(2,128)(2,1)S(1)}, bf16[8,16,2,1024]{3,2,1,0:T(2,128)(2,1)}, u32[]{:S(2)}) copy-start(bf16[8,16,2,1024]{3,2,1,0:T(2,128)(2,1)} %param.35) | copy-start | bytes 1572868
Sparse Core Ops, SparseCore 0:
  78.1 30.4 all-gather.10
  110.2 29.4 all-gather.8
  149.4 28.2 all-gather.14
  179.2 27.3 all-gather.12
